TPU v7x, 32 devices: a whole 2x2x4 slice. The times are simulated.
32 devices in a mesh: groups: 2 (over x), panel: 16 (over z, y, core).
Axes of the slice: x: 2, y: 2, z: 4, core: 2. Of those that a mesh axis runs over, the one named last changes fastest.
Arguments:
- eig_vectors: bfloat16 [5120, 1024], P(('groups', 'panel')), parts along dimension 0, may hold values from -0.1875 to 0.1875
- eig_values: bfloat16 [5120], P(('groups', 'panel')), parts along dimension 0, may hold values from 0.19921875 to 5
- eig_count: int32 [16], P('groups'), parts along dimension 0, may hold values from 128 to 512, as said below
- snp_count: int32 [16], P('groups'), parts along dimension 0, may hold values from 512 to 1024
- zscores: bfloat16 [32, 8, 1024, 128], P(('groups', 'panel')), parts along dimension 0, may hold values from -6 to 6
- samples: bfloat16 [4096], P('groups'), parts along dimension 0, may hold values from 20 to 160
Outputs:
- covariance: float32 [9, 32, 8, 128, 128], P(None, ('groups', 'panel')), parts along dimension 1
There are 2 independent parts, one for each index of `groups`. A program takes and returns all parts, laid end to end along the dimension named above; each array names one. Nothing has to cross between parts.
Inputs may be any that keep to these rules, and one draw needn't show every extreme that they name: `eig_count`: blocks 2m and 2m+1 hold 640 eigenvectors together, so every block group holds 2560; some block holds exactly 512.
All inputs are finite; a program needn't handle non-finite values.
Results may differ from a plain program's by a relative error of at most 0.0045.
Values may be sent and summed in bfloat16 or wider, within the bound.
A program may use at most 64 MiB of HBM per device.

v0:
```python
import jax
import jax.numpy as jnp
from jax import lax
from jax.sharding import PartitionSpec as P

KMAX = 512
ROUNDS = 8


def passed_along(shard, axis, by):
    size = lax.axis_size(axis)
    return lax.ppermute(shard, axis, [(i, (i + by) % size) for i in range(size)])


def project_blocks(vectors, counts, snps, scores):
    offsets = jnp.cumsum(counts) - counts
    row_total = vectors.shape[0]
    positions = jnp.arange(scores.shape[1], dtype=jnp.int32)
    kept = jnp.arange(KMAX, dtype=jnp.int32)

    def one_block(block_index, projected):
        start_row = offsets[block_index]
        live_count = counts[block_index]
        row_start = jnp.minimum(start_row, row_total - KMAX)
        eig_rows = lax.dynamic_slice_in_dim(vectors, row_start, KMAX, 0)
        block_scores = lax.dynamic_index_in_dim(scores, block_index, 0, keepdims=False)
        z_masked = jnp.where(
            (positions < snps[block_index])[:, None], block_scores, jnp.zeros_like(block_scores)
        )
        projection = jnp.dot(eig_rows, z_masked, preferred_element_type=jnp.float32).astype(
            jnp.bfloat16
        )
        row_index = row_start + kept
        keep_rows = (row_index >= start_row) & (row_index < start_row + live_count)
        previous = lax.dynamic_slice_in_dim(projected, row_start, KMAX, 0)
        merged = jnp.where(keep_rows[:, None], projection, previous)
        return lax.dynamic_update_slice_in_dim(projected, merged, row_start, 0)

    initial = jnp.zeros((row_total, scores.shape[2]), jnp.bfloat16)
    return lax.fori_loop(0, counts.shape[0], one_block, initial)


def per_device(eig_vectors, eig_values, eig_count, snp_count, zscores, samples):
    devices = lax.axis_size("panel")
    spacing = max(1, devices // 32)
    panels = devices // spacing
    slot_index = lax.axis_index("panel")
    panel_index = slot_index // spacing
    group_index = slot_index % spacing
    piece_rows = eig_vectors.shape[0]
    snp_rows = eig_vectors.shape[1]
    row_store = jnp.zeros((panels, piece_rows, snp_rows), jnp.bfloat16)
    value_store = jnp.zeros((panels, piece_rows), jnp.bfloat16)
    row_store = lax.dynamic_update_slice_in_dim(row_store, eig_vectors[None], panel_index, 0)
    value_store = lax.dynamic_update_slice_in_dim(value_store, eig_values[None], panel_index, 0)

    def cycle_step(turn_index, carry):
        rows_kept, values_kept, held_rows, held_values = carry
        held_rows, held_values = passed_along((held_rows, held_values), "panel", spacing)
        source = (panel_index - turn_index) % panels
        rows_kept = lax.dynamic_update_slice_in_dim(rows_kept, held_rows[None], source, 0)
        values_kept = lax.dynamic_update_slice_in_dim(values_kept, held_values[None], source, 0)
        return (rows_kept, values_kept, held_rows, held_values)

    row_store, value_store, unused_rows, unused_values = lax.fori_loop(
        1, panels, cycle_step, (row_store, value_store, eig_vectors, eig_values)
    )
    group_vectors = row_store.reshape(panels * piece_rows, snp_rows)
    group_values = value_store.reshape(panels * piece_rows)
    blocks_here = zscores.shape[1]
    panel_width = zscores.shape[3]
    counts = lax.dynamic_slice_in_dim(eig_count, group_index * blocks_here, blocks_here)
    snps = lax.dynamic_slice_in_dim(snp_count, group_index * blocks_here, blocks_here)
    projected = project_blocks(group_vectors, counts, snps, zscores[0])
    weighted = (projected.astype(jnp.float32) / group_values.astype(jnp.float32)[:, None]).astype(
        jnp.bfloat16
    )
    row_total = projected.shape[0]
    offsets = jnp.cumsum(counts) - counts
    kept = jnp.arange(KMAX, dtype=jnp.int32)
    scales_all = samples.astype(jnp.float32)
    own_scale = lax.dynamic_slice_in_dim(scales_all, panel_index * panel_width, panel_width)

    def cross(partner, round_index, first):
        partner_panel = (panel_index - round_index) % panels
        partner_scale = lax.dynamic_slice_in_dim(
            scales_all, partner_panel * panel_width, panel_width
        )
        divisor = jnp.sqrt(own_scale[:, None] * partner_scale[None, :])

        def block_gram(block_index):
            start_row = offsets[block_index]
            row_start = jnp.minimum(start_row, row_total - KMAX)
            row_index = row_start + kept
            keep_rows = (row_index >= start_row) & (row_index < start_row + counts[block_index])
            left_slab = lax.dynamic_slice_in_dim(weighted, row_start, KMAX, 0)
            left_slab = jnp.where(keep_rows[:, None], left_slab, jnp.zeros_like(left_slab))
            right_slab = lax.dynamic_slice_in_dim(partner, row_start, KMAX, 0)
            gram = lax.dot_general(
                left_slab, right_slab, (((0,), (0,)), ((), ())), preferred_element_type=jnp.float32
            )
            if first:
                gram = gram - counts[block_index].astype(jnp.float32) * jnp.eye(
                    panel_width, dtype=jnp.float32
                )
            return gram / divisor

        return lax.map(block_gram, jnp.arange(blocks_here, dtype=jnp.int32))

    results = [cross(projected, 0, True)]
    for round_index in range(1, ROUNDS + 1):
        received = passed_along(projected, "panel", round_index * spacing)
        results.append(cross(received, round_index, False))
    return jnp.stack(results)[:, None]


def solution(mesh):
    placed = (
        P(("groups", "panel"), None),
        P(("groups", "panel")),
        P("groups"),
        P("groups"),
        P(("groups", "panel"), None, None, None),
        P("groups"),
    )
    return jax.shard_map(
        per_device,
        mesh=mesh,
        in_specs=placed,
        out_specs=P(None, ("groups", "panel"), None, None, None),
        check_vma=False,
    )
```

profile of v0, /device:TPU:1, one launch (start us, length us, event | category | flops | bytes accessed | tf_op | source)
XLA Modules:
  0.0 804.5 jit_solution(9370108276213926608)
XLA Ops:
  3.1 3.0 broadcast_in_dim.182
  6.9 144.8 %while.134 = (s32[]{:T(128)}, bf16[16,160,1024]{2,1,0:T(8,128)(2,1)}, bf16[16,160]{1,0:T(8,128)(2,1)S(1)}, bf16[160,1024]{1,0:T(8,128)(2,1)S(1)}, bf16[160]{0:T(...) while((s32[]{:T(128)}, bf16[16,160,1024]{2,1,0:T(8,128)(2,1)}, ...), condition=%wide.region_2.3_spmd, body=%wide.region_1.2_spmd.sunk | while | flops 17 | bytes 2624984 | solution.py:65
  6.9 2.7 collective-permute-start
  9.7 4.0 collective-permute-done.1
  14.5 2.5 collective-permute-start
  17.0 4.0 collective-permute-done.1
  21.9 2.5 collective-permute-start
  24.5 5.0 collective-permute-done.1
  32.8 6.7 collective-permute-done.1
  41.1 8.5 %collective-permute-done.1 = bf16[160]{0:T(256)(128)(2,1)S(1)} collective-permute-done((bf16[160]{0:T(256)(128)(2,1)S(1)}, bf16[160]{0:T(256)(128)(2,1)S(1)}, u32[]{:S(2)}, u32[]{:S(2)}) %collective-permute-start.1) | collective-permute-done | bytes 352 | tf_op jit(solution)/shard_map/while/body/eval_jaxpr/ppermute | solution.py:12
  50.5 9.3 %collective-permute-done.1 = bf16[160]{0:T(256)(128)(2,1)S(1)} collective-permute-done((bf16[160]{0:T(256)(128)(2,1)S(1)}, bf16[160]{0:T(256)(128)(2,1)S(1)}, u32[]{:S(2)}, u32[]{:S(2)}) %collective-permute-start.1) | collective-permute-done | bytes 352 | tf_op jit(solution)/shard_map/while/body/eval_jaxpr/ppermute | solution.py:12
  60.6 9.3 %collective-permute-done.1 = bf16[160]{0:T(256)(128)(2,1)S(1)} collective-permute-done((bf16[160]{0:T(256)(128)(2,1)S(1)}, bf16[160]{0:T(256)(128)(2,1)S(1)}, u32[]{:S(2)}, u32[]{:S(2)}) %collective-permute-start.1) | collective-permute-done | bytes 352 | tf_op jit(solution)/shard_map/while/body/eval_jaxpr/ppermute | solution.py:12
  70.7 9.3 %collective-permute-done.1 = bf16[160]{0:T(256)(128)(2,1)S(1)} collective-permute-done((bf16[160]{0:T(256)(128)(2,1)S(1)}, bf16[160]{0:T(256)(128)(2,1)S(1)}, u32[]{:S(2)}, u32[]{:S(2)}) %collective-permute-start.1) | collective-permute-done | bytes 352 | tf_op jit(solution)/shard_map/while/body/eval_jaxpr/ppermute | solution.py:12
  80.8 9.3 %collective-permute-done.1 = bf16[160]{0:T(256)(128)(2,1)S(1)} collective-permute-done((bf16[160]{0:T(256)(128)(2,1)S(1)}, bf16[160]{0:T(256)(128)(2,1)S(1)}, u32[]{:S(2)}, u32[]{:S(2)}) %collective-permute-start.1) | collective-permute-done | bytes 352 | tf_op jit(solution)/shard_map/while/body/eval_jaxpr/ppermute | solution.py:12
  91.0 9.3 %collective-permute-done.1 = bf16[160]{0:T(256)(128)(2,1)S(1)} collective-permute-done((bf16[160]{0:T(256)(128)(2,1)S(1)}, bf16[160]{0:T(256)(128)(2,1)S(1)}, u32[]{:S(2)}, u32[]{:S(2)}) %collective-permute-start.1) | collective-permute-done | bytes 352 | tf_op jit(solution)/shard_map/while/body/eval_jaxpr/ppermute | solution.py:12
  101.1 9.3 %collective-permute-done.1 = bf16[160]{0:T(256)(128)(2,1)S(1)} collective-permute-done((bf16[160]{0:T(256)(128)(2,1)S(1)}, bf16[160]{0:T(256)(128)(2,1)S(1)}, u32[]{:S(2)}, u32[]{:S(2)}) %collective-permute-start.1) | collective-permute-done | bytes 352 | tf_op jit(solution)/shard_map/while/body/eval_jaxpr/ppermute | solution.py:12
  111.2 9.3 %collective-permute-done.1 = bf16[160]{0:T(256)(128)(2,1)S(1)} collective-permute-done((bf16[160]{0:T(256)(128)(2,1)S(1)}, bf16[160]{0:T(256)(128)(2,1)S(1)}, u32[]{:S(2)}, u32[]{:S(2)}) %collective-permute-start.1) | collective-permute-done | bytes 352 | tf_op jit(solution)/shard_map/while/body/eval_jaxpr/ppermute | solution.py:12
  121.4 9.3 %collective-permute-done.1 = bf16[160]{0:T(256)(128)(2,1)S(1)} collective-permute-done((bf16[160]{0:T(256)(128)(2,1)S(1)}, bf16[160]{0:T(256)(128)(2,1)S(1)}, u32[]{:S(2)}, u32[]{:S(2)}) %collective-permute-start.1) | collective-permute-done | bytes 352 | tf_op jit(solution)/shard_map/while/body/eval_jaxpr/ppermute | solution.py:12
  131.5 9.3 %collective-permute-done.1 = bf16[160]{0:T(256)(128)(2,1)S(1)} collective-permute-done((bf16[160]{0:T(256)(128)(2,1)S(1)}, bf16[160]{0:T(256)(128)(2,1)S(1)}, u32[]{:S(2)}, u32[]{:S(2)}) %collective-permute-start.1) | collective-permute-done | bytes 352 | tf_op jit(solution)/shard_map/while/body/eval_jaxpr/ppermute | solution.py:12
  141.6 9.3 %collective-permute-done.1 = bf16[160]{0:T(256)(128)(2,1)S(1)} collective-permute-done((bf16[160]{0:T(256)(128)(2,1)S(1)}, bf16[160]{0:T(256)(128)(2,1)S(1)}, u32[]{:S(2)}, u32[]{:S(2)}) %collective-permute-start.1) | collective-permute-done | bytes 352 | tf_op jit(solution)/shard_map/while/body/eval_jaxpr/ppermute | solution.py:12
  152.7 67.7 %while.135 = (s32[]{:T(128)}, bf16[2560,128]{1,0:T(8,128)(2,1)}, s32[8]{0:T(128)S(1)}, s32[8]{0:T(128)S(1)}, bf16[2560,1024]{1,0:T(8,128)(2,1)}, /*index=5*/s32[...) while((s32[]{:T(128)}, bf16[2560,128]{1,0:T(8,128)(2,1)}, ...), condition=%wide.region_4.5_spmd.clone, body=%wide.region_3.4_spmd.clone.sunk | while | flops 134482944 | bytes 1839839 | solution.py:40
  220.5 13.3 %collective-permute-start.6 = (bf16[2560,128]{1,0:T(8,128)(2,1)}, bf16[2560,128]{1,0:T(8,128)(2,1)}, u32[]{:S(2)}, u32[]{:S(2)}) collective-permute-start(bf16[2560,128]{1,0:T(8,128)(2,1)} %get-tuple-element.1816), channel_id=1, source_target_pairs={{0,5},{1,6},{2,7},{3,8},{4,9},{5,10},{6,11},{7,12},{8,13},{9,14},{... | collective-permute-start | bytes 1966088 | tf_op jit(solution)/shard_map/ppermute | solution.py:12
  235.6 60.9 %while.136 = (s32[]{:T(128)}, f32[8,128,128]{2,1,0:T(8,128)S(1)}, s32[8]{0:T(128)S(1)}, s32[8]{0:T(128)S(1)}, s32[8]{0:T(128)S(1)}, /*index=5*/bf16[2560,128]{1,...) while((s32[]{:T(128)}, f32[8,128,128]{2,1,0:T(8,128)S(1)}, ...), condition=%wide.region_6.7_spmd.clone, body=%wide.region_5.6_spmd.clone.sunk | while | flops 16926732 | bytes 332057 | solution.py:108
  297.4 57.5 %while.139 = (s32[]{:T(128)}, f32[8,128,128]{2,1,0:T(8,128)S(1)}, s32[8]{0:T(128)S(1)}, s32[8]{0:T(128)S(1)}, s32[8]{0:T(128)S(1)}, /*index=5*/bf16[2560,128]{1,...) while((s32[]{:T(128)}, f32[8,128,128]{2,1,0:T(8,128)S(1)}, ...), condition=%wide.region_12.13_spmd.clone, body=%wide.region_11.12_spmd.clone.sunk | while | flops 16877576 | bytes 331537 | solution.py:108
  355.0 63.6 %while.138 = (s32[]{:T(128)}, f32[8,128,128]{2,1,0:T(8,128)S(1)}, s32[8]{0:T(128)S(1)}, s32[8]{0:T(128)S(1)}, s32[8]{0:T(128)S(1)}, /*index=5*/bf16[2560,128]{1,...) while((s32[]{:T(128)}, f32[8,128,128]{2,1,0:T(8,128)S(1)}, ...), condition=%wide.region_10.11_spmd.clone, body=%wide.region_9.10_spmd.clone.sunk | while | flops 16877576 | bytes 331537 | solution.py:108
  418.7 2.7 collective-permute-start.9
  421.4 53.1 %while.137 = (s32[]{:T(128)}, f32[8,128,128]{2,1,0:T(8,128)S(1)}, s32[8]{0:T(128)S(1)}, s32[8]{0:T(128)S(1)}, s32[8]{0:T(128)S(1)}, /*index=5*/bf16[2560,128]{1,...) while((s32[]{:T(128)}, f32[8,128,128]{2,1,0:T(8,128)S(1)}, ...), condition=%wide.region_8.9_spmd.clone, body=%wide.region_7.8_spmd.clone.sunk | while | flops 16877576 | bytes 331029 | solution.py:108
  474.6 60.1 %while.140 = (s32[]{:T(128)}, f32[8,128,128]{2,1,0:T(8,128)S(1)}, s32[8]{0:T(128)S(1)}, s32[8]{0:T(128)S(1)}, s32[8]{0:T(128)S(1)}, /*index=5*/bf16[2560,128]{1,...) while((s32[]{:T(128)}, f32[8,128,128]{2,1,0:T(8,128)S(1)}, ...), condition=%wide.region_14.15_spmd.clone, body=%wide.region_13.14_spmd.clone.sunk | while | flops 16877576 | bytes 331537 | solution.py:108
  534.8 63.6 %while.141 = (s32[]{:T(128)}, f32[8,128,128]{2,1,0:T(8,128)S(1)}, s32[8]{0:T(128)S(1)}, s32[8]{0:T(128)S(1)}, s32[8]{0:T(128)S(1)}, /*index=5*/bf16[2560,128]{1,...) while((s32[]{:T(128)}, f32[8,128,128]{2,1,0:T(8,128)S(1)}, ...), condition=%wide.region_16.17_spmd.clone, body=%wide.region_15.16_spmd.clone.sunk | while | flops 16877576 | bytes 331537 | solution.py:108
  599.3 64.1 %while.142 = (s32[]{:T(128)}, f32[8,128,128]{2,1,0:T(8,128)S(1)}, s32[8]{0:T(128)S(1)}, s32[8]{0:T(128)S(1)}, s32[8]{0:T(128)S(1)}, /*index=5*/bf16[2560,128]{1,...) while((s32[]{:T(128)}, f32[8,128,128]{2,1,0:T(8,128)S(1)}, ...), condition=%wide.region_18.19_spmd.clone, body=%wide.region_17.18_spmd.clone.sunk | while | flops 16877576 | bytes 331537 | solution.py:108
  664.4 69.0 %while.143 = (s32[]{:T(128)}, f32[8,128,128]{2,1,0:T(8,128)}, s32[8]{0:T(128)S(1)}, s32[8]{0:T(128)S(1)}, s32[8]{0:T(128)S(1)}, /*index=5*/bf16[2560,128]{1,0:T(...) while((s32[]{:T(128)}, f32[8,128,128]{2,1,0:T(8,128)}, ...), condition=%wide.region_20.21_spmd.clone, body=%wide.region_19.20_spmd.clone.sunk | while | flops 16877576 | bytes 331537 | solution.py:108
  733.4 64.4 %while.144 = (s32[]{:T(128)}, f32[8,128,128]{2,1,0:T(8,128)S(1)}, s32[8]{0:T(128)S(1)}, s32[8]{0:T(128)S(1)}, s32[8]{0:T(128)S(1)}, /*index=5*/bf16[2560,128]{1,...) while((s32[]{:T(128)}, f32[8,128,128]{2,1,0:T(8,128)S(1)}, ...), condition=%wide.region_22.23_spmd.clone, body=%wide.region_21.22_spmd.clone.sunk | while | flops 16877576 | bytes 331537 | solution.py:108
  (600 shorter events, 356.9 us)
Async XLA Ops:
  30.3 9.3 %collective-permute-start = (bf16[160,1024]{1,0:T(8,128)(2,1)S(1)}, bf16[160,1024]{1,0:T(8,128)(2,1)S(1)}, u32[]{:S(2)}, u32[]{:S(2)}) collective-permute-start(bf16[160,1024]{1,0:T(8,128)(2,1)S(1)} %get-tuple-element.1760), channel_id=1, source_target_pairs={{0,1},{1,2},{2,3},{3,4},{4,5},{5,6},{6,7},{7,8},{8,9},{9,10},{10,1... | collective-permute-start | bytes 983048 | tf_op jit(solution)/shard_map/while/body/eval_jaxpr/ppermute | solution.py:12
  31.9 7.7 collective-permute-start.1
  40.3 9.3 %collective-permute-start = (bf16[160,1024]{1,0:T(8,128)(2,1)S(1)}, bf16[160,1024]{1,0:T(8,128)(2,1)S(1)}, u32[]{:S(2)}, u32[]{:S(2)}) collective-permute-start(bf16[160,1024]{1,0:T(8,128)(2,1)S(1)} %get-tuple-element.1760), channel_id=1, source_target_pairs={{0,1},{1,2},{2,3},{3,4},{4,5},{5,6},{6,7},{7,8},{8,9},{9,10},{10,1... | collective-permute-start | bytes 983048 | tf_op jit(solution)/shard_map/while/body/eval_jaxpr/ppermute | solution.py:12
  40.3 9.3 %collective-permute-start.1 = (bf16[160]{0:T(256)(128)(2,1)S(1)}, bf16[160]{0:T(256)(128)(2,1)S(1)}, u32[]{:S(2)}, u32[]{:S(2)}) collective-permute-start(bf16[160]{0:T(256)(128)(2,1)S(1)} %get-tuple-element.1761), channel_id=1, source_target_pairs={{0,1},{1,2},{2,3},{3,4},{4,5},{5,6},{6,7},{7,8},{8,9},{9,10},{10,1... | collective-permute-start | bytes 968 | tf_op jit(solution)/shard_map/while/body/eval_jaxpr/ppermute | solution.py:12
  50.5 9.3 %collective-permute-start = (bf16[160,1024]{1,0:T(8,128)(2,1)S(1)}, bf16[160,1024]{1,0:T(8,128)(2,1)S(1)}, u32[]{:S(2)}, u32[]{:S(2)}) collective-permute-start(bf16[160,1024]{1,0:T(8,128)(2,1)S(1)} %get-tuple-element.1760), channel_id=1, source_target_pairs={{0,1},{1,2},{2,3},{3,4},{4,5},{5,6},{6,7},{7,8},{8,9},{9,10},{10,1... | collective-permute-start | bytes 983048 | tf_op jit(solution)/shard_map/while/body/eval_jaxpr/ppermute | solution.py:12
  50.5 9.3 %collective-permute-start.1 = (bf16[160]{0:T(256)(128)(2,1)S(1)}, bf16[160]{0:T(256)(128)(2,1)S(1)}, u32[]{:S(2)}, u32[]{:S(2)}) collective-permute-start(bf16[160]{0:T(256)(128)(2,1)S(1)} %get-tuple-element.1761), channel_id=1, source_target_pairs={{0,1},{1,2},{2,3},{3,4},{4,5},{5,6},{6,7},{7,8},{8,9},{9,10},{10,1... | collective-permute-start | bytes 968 | tf_op jit(solution)/shard_map/while/body/eval_jaxpr/ppermute | solution.py:12
  60.6 9.3 %collective-permute-start = (bf16[160,1024]{1,0:T(8,128)(2,1)S(1)}, bf16[160,1024]{1,0:T(8,128)(2,1)S(1)}, u32[]{:S(2)}, u32[]{:S(2)}) collective-permute-start(bf16[160,1024]{1,0:T(8,128)(2,1)S(1)} %get-tuple-element.1760), channel_id=1, source_target_pairs={{0,1},{1,2},{2,3},{3,4},{4,5},{5,6},{6,7},{7,8},{8,9},{9,10},{10,1... | collective-permute-start | bytes 983048 | tf_op jit(solution)/shard_map/while/body/eval_jaxpr/ppermute | solution.py:12
  60.6 9.3 %collective-permute-start.1 = (bf16[160]{0:T(256)(128)(2,1)S(1)}, bf16[160]{0:T(256)(128)(2,1)S(1)}, u32[]{:S(2)}, u32[]{:S(2)}) collective-permute-start(bf16[160]{0:T(256)(128)(2,1)S(1)} %get-tuple-element.1761), channel_id=1, source_target_pairs={{0,1},{1,2},{2,3},{3,4},{4,5},{5,6},{6,7},{7,8},{8,9},{9,10},{10,1... | collective-permute-start | bytes 968 | tf_op jit(solution)/shard_map/while/body/eval_jaxpr/ppermute | solution.py:12
  70.7 9.3 %collective-permute-start = (bf16[160,1024]{1,0:T(8,128)(2,1)S(1)}, bf16[160,1024]{1,0:T(8,128)(2,1)S(1)}, u32[]{:S(2)}, u32[]{:S(2)}) collective-permute-start(bf16[160,1024]{1,0:T(8,128)(2,1)S(1)} %get-tuple-element.1760), channel_id=1, source_target_pairs={{0,1},{1,2},{2,3},{3,4},{4,5},{5,6},{6,7},{7,8},{8,9},{9,10},{10,1... | collective-permute-start | bytes 983048 | tf_op jit(solution)/shard_map/while/body/eval_jaxpr/ppermute | solution.py:12
  70.7 9.3 %collective-permute-start.1 = (bf16[160]{0:T(256)(128)(2,1)S(1)}, bf16[160]{0:T(256)(128)(2,1)S(1)}, u32[]{:S(2)}, u32[]{:S(2)}) collective-permute-start(bf16[160]{0:T(256)(128)(2,1)S(1)} %get-tuple-element.1761), channel_id=1, source_target_pairs={{0,1},{1,2},{2,3},{3,4},{4,5},{5,6},{6,7},{7,8},{8,9},{9,10},{10,1... | collective-permute-start | bytes 968 | tf_op jit(solution)/shard_map/while/body/eval_jaxpr/ppermute | solution.py:12
  80.8 9.3 %collective-permute-start = (bf16[160,1024]{1,0:T(8,128)(2,1)S(1)}, bf16[160,1024]{1,0:T(8,128)(2,1)S(1)}, u32[]{:S(2)}, u32[]{:S(2)}) collective-permute-start(bf16[160,1024]{1,0:T(8,128)(2,1)S(1)} %get-tuple-element.1760), channel_id=1, source_target_pairs={{0,1},{1,2},{2,3},{3,4},{4,5},{5,6},{6,7},{7,8},{8,9},{9,10},{10,1... | collective-permute-start | bytes 983048 | tf_op jit(solution)/shard_map/while/body/eval_jaxpr/ppermute | solution.py:12
  80.8 9.3 %collective-permute-start.1 = (bf16[160]{0:T(256)(128)(2,1)S(1)}, bf16[160]{0:T(256)(128)(2,1)S(1)}, u32[]{:S(2)}, u32[]{:S(2)}) collective-permute-start(bf16[160]{0:T(256)(128)(2,1)S(1)} %get-tuple-element.1761), channel_id=1, source_target_pairs={{0,1},{1,2},{2,3},{3,4},{4,5},{5,6},{6,7},{7,8},{8,9},{9,10},{10,1... | collective-permute-start | bytes 968 | tf_op jit(solution)/shard_map/while/body/eval_jaxpr/ppermute | solution.py:12
  91.0 9.3 %collective-permute-start = (bf16[160,1024]{1,0:T(8,128)(2,1)S(1)}, bf16[160,1024]{1,0:T(8,128)(2,1)S(1)}, u32[]{:S(2)}, u32[]{:S(2)}) collective-permute-start(bf16[160,1024]{1,0:T(8,128)(2,1)S(1)} %get-tuple-element.1760), channel_id=1, source_target_pairs={{0,1},{1,2},{2,3},{3,4},{4,5},{5,6},{6,7},{7,8},{8,9},{9,10},{10,1... | collective-permute-start | bytes 983048 | tf_op jit(solution)/shard_map/while/body/eval_jaxpr/ppermute | solution.py:12
  91.0 9.3 %collective-permute-start.1 = (bf16[160]{0:T(256)(128)(2,1)S(1)}, bf16[160]{0:T(256)(128)(2,1)S(1)}, u32[]{:S(2)}, u32[]{:S(2)}) collective-permute-start(bf16[160]{0:T(256)(128)(2,1)S(1)} %get-tuple-element.1761), channel_id=1, source_target_pairs={{0,1},{1,2},{2,3},{3,4},{4,5},{5,6},{6,7},{7,8},{8,9},{9,10},{10,1... | collective-permute-start | bytes 968 | tf_op jit(solution)/shard_map/while/body/eval_jaxpr/ppermute | solution.py:12
  101.1 9.3 %collective-permute-start = (bf16[160,1024]{1,0:T(8,128)(2,1)S(1)}, bf16[160,1024]{1,0:T(8,128)(2,1)S(1)}, u32[]{:S(2)}, u32[]{:S(2)}) collective-permute-start(bf16[160,1024]{1,0:T(8,128)(2,1)S(1)} %get-tuple-element.1760), channel_id=1, source_target_pairs={{0,1},{1,2},{2,3},{3,4},{4,5},{5,6},{6,7},{7,8},{8,9},{9,10},{10,1... | collective-permute-start | bytes 983048 | tf_op jit(solution)/shard_map/while/body/eval_jaxpr/ppermute | solution.py:12
  101.1 9.3 %collective-permute-start.1 = (bf16[160]{0:T(256)(128)(2,1)S(1)}, bf16[160]{0:T(256)(128)(2,1)S(1)}, u32[]{:S(2)}, u32[]{:S(2)}) collective-permute-start(bf16[160]{0:T(256)(128)(2,1)S(1)} %get-tuple-element.1761), channel_id=1, source_target_pairs={{0,1},{1,2},{2,3},{3,4},{4,5},{5,6},{6,7},{7,8},{8,9},{9,10},{10,1... | collective-permute-start | bytes 968 | tf_op jit(solution)/shard_map/while/body/eval_jaxpr/ppermute | solution.py:12
  111.2 9.4 %collective-permute-start = (bf16[160,1024]{1,0:T(8,128)(2,1)S(1)}, bf16[160,1024]{1,0:T(8,128)(2,1)S(1)}, u32[]{:S(2)}, u32[]{:S(2)}) collective-permute-start(bf16[160,1024]{1,0:T(8,128)(2,1)S(1)} %get-tuple-element.1760), channel_id=1, source_target_pairs={{0,1},{1,2},{2,3},{3,4},{4,5},{5,6},{6,7},{7,8},{8,9},{9,10},{10,1... | collective-permute-start | bytes 983048 | tf_op jit(solution)/shard_map/while/body/eval_jaxpr/ppermute | solution.py:12
  111.2 9.3 %collective-permute-start.1 = (bf16[160]{0:T(256)(128)(2,1)S(1)}, bf16[160]{0:T(256)(128)(2,1)S(1)}, u32[]{:S(2)}, u32[]{:S(2)}) collective-permute-start(bf16[160]{0:T(256)(128)(2,1)S(1)} %get-tuple-element.1761), channel_id=1, source_target_pairs={{0,1},{1,2},{2,3},{3,4},{4,5},{5,6},{6,7},{7,8},{8,9},{9,10},{10,1... | collective-permute-start | bytes 968 | tf_op jit(solution)/shard_map/while/body/eval_jaxpr/ppermute | solution.py:12
  121.4 9.3 %collective-permute-start = (bf16[160,1024]{1,0:T(8,128)(2,1)S(1)}, bf16[160,1024]{1,0:T(8,128)(2,1)S(1)}, u32[]{:S(2)}, u32[]{:S(2)}) collective-permute-start(bf16[160,1024]{1,0:T(8,128)(2,1)S(1)} %get-tuple-element.1760), channel_id=1, source_target_pairs={{0,1},{1,2},{2,3},{3,4},{4,5},{5,6},{6,7},{7,8},{8,9},{9,10},{10,1... | collective-permute-start | bytes 983048 | tf_op jit(solution)/shard_map/while/body/eval_jaxpr/ppermute | solution.py:12
  121.4 9.3 %collective-permute-start.1 = (bf16[160]{0:T(256)(128)(2,1)S(1)}, bf16[160]{0:T(256)(128)(2,1)S(1)}, u32[]{:S(2)}, u32[]{:S(2)}) collective-permute-start(bf16[160]{0:T(256)(128)(2,1)S(1)} %get-tuple-element.1761), channel_id=1, source_target_pairs={{0,1},{1,2},{2,3},{3,4},{4,5},{5,6},{6,7},{7,8},{8,9},{9,10},{10,1... | collective-permute-start | bytes 968 | tf_op jit(solution)/shard_map/while/body/eval_jaxpr/ppermute | solution.py:12
  131.5 9.3 %collective-permute-start = (bf16[160,1024]{1,0:T(8,128)(2,1)S(1)}, bf16[160,1024]{1,0:T(8,128)(2,1)S(1)}, u32[]{:S(2)}, u32[]{:S(2)}) collective-permute-start(bf16[160,1024]{1,0:T(8,128)(2,1)S(1)} %get-tuple-element.1760), channel_id=1, source_target_pairs={{0,1},{1,2},{2,3},{3,4},{4,5},{5,6},{6,7},{7,8},{8,9},{9,10},{10,1... | collective-permute-start | bytes 983048 | tf_op jit(solution)/shard_map/while/body/eval_jaxpr/ppermute | solution.py:12
  131.5 9.3 %collective-permute-start.1 = (bf16[160]{0:T(256)(128)(2,1)S(1)}, bf16[160]{0:T(256)(128)(2,1)S(1)}, u32[]{:S(2)}, u32[]{:S(2)}) collective-permute-start(bf16[160]{0:T(256)(128)(2,1)S(1)} %get-tuple-element.1761), channel_id=1, source_target_pairs={{0,1},{1,2},{2,3},{3,4},{4,5},{5,6},{6,7},{7,8},{8,9},{9,10},{10,1... | collective-permute-start | bytes 968 | tf_op jit(solution)/shard_map/while/body/eval_jaxpr/ppermute | solution.py:12
  141.6 9.3 %collective-permute-start = (bf16[160,1024]{1,0:T(8,128)(2,1)S(1)}, bf16[160,1024]{1,0:T(8,128)(2,1)S(1)}, u32[]{:S(2)}, u32[]{:S(2)}) collective-permute-start(bf16[160,1024]{1,0:T(8,128)(2,1)S(1)} %get-tuple-element.1760), channel_id=1, source_target_pairs={{0,1},{1,2},{2,3},{3,4},{4,5},{5,6},{6,7},{7,8},{8,9},{9,10},{10,1... | collective-permute-start | bytes 983048 | tf_op jit(solution)/shard_map/while/body/eval_jaxpr/ppermute | solution.py:12
  141.6 9.3 %collective-permute-start.1 = (bf16[160]{0:T(256)(128)(2,1)S(1)}, bf16[160]{0:T(256)(128)(2,1)S(1)}, u32[]{:S(2)}, u32[]{:S(2)}) collective-permute-start(bf16[160]{0:T(256)(128)(2,1)S(1)} %get-tuple-element.1761), channel_id=1, source_target_pairs={{0,1},{1,2},{2,3},{3,4},{4,5},{5,6},{6,7},{7,8},{8,9},{9,10},{10,1... | collective-permute-start | bytes 968 | tf_op jit(solution)/shard_map/while/body/eval_jaxpr/ppermute | solution.py:12
  220.4 77.0 %collective-permute-start.4 = (bf16[2560,128]{1,0:T(8,128)(2,1)}, bf16[2560,128]{1,0:T(8,128)(2,1)}, u32[]{:S(2)}, u32[]{:S(2)}) collective-permute-start(bf16[2560,128]{1,0:T(8,128)(2,1)} %get-tuple-element.1816), channel_id=1, source_target_pairs={{0,3},{1,4},{2,5},{3,6},{4,7},{5,8},{6,9},{7,10},{8,11},{9,12},{10... | collective-permute-start | bytes 1966088 | tf_op jit(solution)/shard_map/ppermute | solution.py:12
  220.4 134.6 %collective-permute-start.3 = (bf16[2560,128]{1,0:T(8,128)(2,1)}, bf16[2560,128]{1,0:T(8,128)(2,1)}, u32[]{:S(2)}, u32[]{:S(2)}) collective-permute-start(bf16[2560,128]{1,0:T(8,128)(2,1)} %get-tuple-element.1816), channel_id=1, source_target_pairs={{0,2},{1,3},{2,4},{3,5},{4,6},{5,7},{6,8},{7,9},{8,10},{9,11},{10,... | collective-permute-start | bytes 1966088 | tf_op jit(solution)/shard_map/ppermute | solution.py:12
  220.4 198.3 %collective-permute-start.2 = (bf16[2560,128]{1,0:T(8,128)(2,1)}, bf16[2560,128]{1,0:T(8,128)(2,1)S(1)}, u32[]{:S(2)}, u32[]{:S(2)}) collective-permute-start(bf16[2560,128]{1,0:T(8,128)(2,1)} %get-tuple-element.1816), channel_id=1, source_target_pairs={{0,1},{1,2},{2,3},{3,4},{4,5},{5,6},{6,7},{7,8},{8,9},{9,10},{10,1... | collective-permute-start | bytes 1966088 | tf_op jit(solution)/shard_map/ppermute | solution.py:12
  220.4 254.1 %collective-permute-start.5 = (bf16[2560,128]{1,0:T(8,128)(2,1)}, bf16[2560,128]{1,0:T(8,128)(2,1)}, u32[]{:S(2)}, u32[]{:S(2)}) collective-permute-start(bf16[2560,128]{1,0:T(8,128)(2,1)} %get-tuple-element.1816), channel_id=1, source_target_pairs={{0,4},{1,5},{2,6},{3,7},{4,8},{5,9},{6,10},{7,11},{8,12},{9,13},{1... | collective-permute-start | bytes 1966088 | tf_op jit(solution)/shard_map/ppermute | solution.py:12
  220.5 314.3 %collective-permute-start.6 = (bf16[2560,128]{1,0:T(8,128)(2,1)}, bf16[2560,128]{1,0:T(8,128)(2,1)}, u32[]{:S(2)}, u32[]{:S(2)}) collective-permute-start(bf16[2560,128]{1,0:T(8,128)(2,1)} %get-tuple-element.1816), channel_id=1, source_target_pairs={{0,5},{1,6},{2,7},{3,8},{4,9},{5,10},{6,11},{7,12},{8,13},{9,14},{... | collective-permute-start | bytes 1966088 | tf_op jit(solution)/shard_map/ppermute | solution.py:12
  297.4 301.1 %collective-permute-start.7 = (bf16[2560,128]{1,0:T(8,128)(2,1)}, bf16[2560,128]{1,0:T(8,128)(2,1)}, u32[]{:S(2)}, u32[]{:S(2)}) collective-permute-start(bf16[2560,128]{1,0:T(8,128)(2,1)} %get-tuple-element.1816), channel_id=1, source_target_pairs={{0,6},{1,7},{2,8},{3,9},{4,10},{5,11},{6,12},{7,13},{8,14},{9,15},... | collective-permute-start | bytes 1966088 | tf_op jit(solution)/shard_map/ppermute | solution.py:12
  354.9 308.5 %collective-permute-start.8 = (bf16[2560,128]{1,0:T(8,128)(2,1)}, bf16[2560,128]{1,0:T(8,128)(2,1)}, u32[]{:S(2)}, u32[]{:S(2)}) collective-permute-start(bf16[2560,128]{1,0:T(8,128)(2,1)} %get-tuple-element.1816), channel_id=1, source_target_pairs={{0,7},{1,8},{2,9},{3,10},{4,11},{5,12},{6,13},{7,14},{8,15},{9,0},... | collective-permute-start | bytes 1966088 | tf_op jit(solution)/shard_map/ppermute | solution.py:12
  418.7 314.7 %collective-permute-start.9 = (bf16[2560,128]{1,0:T(8,128)(2,1)}, bf16[2560,128]{1,0:T(8,128)(2,1)}, u32[]{:S(2)}, u32[]{:S(2)}) collective-permute-start(bf16[2560,128]{1,0:T(8,128)(2,1)} %get-tuple-element.1816), channel_id=1, source_target_pairs={{0,8},{1,9},{2,10},{3,11},{4,12},{5,13},{6,14},{7,15},{8,0},{9,1},... | collective-permute-start | bytes 1966088 | tf_op jit(solution)/shard_map/ppermute | solution.py:12
  (13 other events, 489.8 us)
where the time goes:
time: 812 us; the launch traced here: 805 us
  loops' own time  299 us (37%)
  local copies, waits for them, and re-layouts  192 us (24%)
  waiting for transfers between devices  121 us (15%)
  matrix products  105 us (13%)
  other arithmetic  58.6 us (7%)
  starting transfers between devices  27.3 us (3%)
    another operation x9, loops' own time, cross(): return lax.map(block_gram, jnp.arange(blocks_here, dtype=jnp.int32))  284 us
    ppermute x38, waiting for transfers between devices, passed_along(): lax.ppermute(shard, axis, [(i, (i + by) % size) for i in range(size)])  121 us
    dot_general x72, matrix products, block_gram(): lax.dot_general(left_slab, right_slab, (((0,), (0,)), ((), ())), preferre...  90.3 us
    and x72, other arithmetic, block_gram(): (row_index >= start_row) & (row_index < start_row + counts[block_index])  46.5 us
    dynamic_slice x72, local copies, waits for them, and re-layouts, block_gram(): start_row = offsets[block_index]  45.6 us
    dynamic_slice x72, local copies, waits for them, and re-layouts, cross(): return lax.map(block_gram, jnp.arange(blocks_here, dtype=jnp.int32))  45.5 us
    dynamic_slice x72, local copies, waits for them, and re-layouts, block_gram(): counts[block_index]  44.2 us
    ppermute x38, starting transfers between devices, passed_along(): lax.ppermute(shard, axis, [(i, (i + by) % size) for i in range(size)])  27.3 us
  transfers between devices with their start and end apart: 38, of which 15 were waited for; matrix products, arithmetic and copies ran while one was open for 30% of the time, Pallas kernels for 0%

commit v1 on v0

v1 whole, which is shorter than its diff:
```python
import functools

import jax
import jax.numpy as jnp
from jax import lax
from jax.experimental import pallas as pl
from jax.experimental.pallas import tpu as pltpu
from jax.sharding import PartitionSpec as P

KMAX = 512
ROUNDS = 8
ALIGN = 16
LIMIT = 56 * 1024 * 1024


def project_kernel(starts, offsets, counts, snps, vectors, scores, out):
    block = pl.program_id(0)
    slab = min(out.shape[0], KMAX + ALIGN)
    start = pl.multiple_of(starts[block], ALIGN)
    low = offsets[block]
    snp_rows = lax.broadcasted_iota(jnp.int32, scores.shape[2:], 0)
    masked = jnp.where(snp_rows < snps[block], scores[0, 0].astype(jnp.float32), 0.0)
    masked = masked.astype(jnp.bfloat16)
    value = jnp.dot(vectors[pl.ds(start, slab), :], masked, preferred_element_type=jnp.float32)
    rows = start + lax.broadcasted_iota(jnp.int32, value.shape, 0)
    keep = (rows >= low) & (rows < low + counts[block])
    previous = out[pl.ds(start, slab), :].astype(jnp.float32)
    out[pl.ds(start, slab), :] = jnp.where(keep, value, previous).astype(out.dtype)


def project(vectors, scores, starts, offsets, counts, snps):
    row_total = vectors.shape[0]
    blocks, snp_rows, width = scores.shape[1:]
    return pl.pallas_call(
        project_kernel,
        out_shape=jax.ShapeDtypeStruct((row_total, width), jnp.bfloat16),
        grid_spec=pltpu.PrefetchScalarGridSpec(
            num_scalar_prefetch=4,
            grid=(blocks,),
            in_specs=[
                pl.BlockSpec(vectors.shape, lambda b, *_: (0, 0)),
                pl.BlockSpec((1, 1, snp_rows, width), lambda b, *_: (0, b, 0, 0)),
            ],
            out_specs=pl.BlockSpec((row_total, width), lambda b, *_: (0, 0)),
        ),
        compiler_params=pltpu.CompilerParams(vmem_limit_bytes=LIMIT),
    )(starts, offsets, counts, snps, vectors, scores)


def gram_kernel(starts, offsets, counts, slots, weighted, panels, scale, out):
    block = pl.program_id(0)
    slab = min(weighted.shape[0], KMAX + ALIGN)
    width = weighted.shape[1]
    start = pl.multiple_of(starts[block], ALIGN)
    low = offsets[block]
    count = counts[block]
    left = weighted[pl.ds(start, slab), :].astype(jnp.float32)
    rows = start + lax.broadcasted_iota(jnp.int32, left.shape, 0)
    keep = (rows >= low) & (rows < low + count)
    left = jnp.where(keep, left, 0.0).T.astype(jnp.bfloat16)
    for index in range(out.shape[0]):
        right = panels[slots[index], pl.ds(start, slab), :]
        gram = jnp.dot(left, right, preferred_element_type=jnp.float32)
        if index == 0:
            shape = (width, width)
            same = lax.broadcasted_iota(jnp.int32, shape, 0) == lax.broadcasted_iota(
                jnp.int32, shape, 1
            )
            gram = gram - jnp.where(same, count.astype(jnp.float32), 0.0)
        out[index, 0, 0] = gram * scale[index]


def grams(weighted, panels, scale, slots, starts, offsets, counts):
    blocks = counts.shape[0]
    rounds, width = scale.shape[:2]
    return pl.pallas_call(
        gram_kernel,
        out_shape=jax.ShapeDtypeStruct((rounds, 1, blocks, width, width), jnp.float32),
        grid_spec=pltpu.PrefetchScalarGridSpec(
            num_scalar_prefetch=4,
            grid=(blocks,),
            in_specs=[
                pl.BlockSpec(weighted.shape, lambda b, *_: (0, 0), pipeline_mode=pl.Buffered(1)),
                pl.BlockSpec(panels.shape, lambda b, *_: (0, 0, 0), pipeline_mode=pl.Buffered(1)),
                pl.BlockSpec(scale.shape, lambda b, *_: (0, 0, 0), pipeline_mode=pl.Buffered(1)),
            ],
            out_specs=pl.BlockSpec((rounds, 1, 1, width, width), lambda b, *_: (0, 0, b, 0, 0)),
        ),
        compiler_params=pltpu.CompilerParams(vmem_limit_bytes=LIMIT),
    )(starts, offsets, counts, slots, weighted, panels, scale)


def per_device(eig_vectors, eig_values, eig_count, snp_count, zscores, samples):
    devices = lax.axis_size("panel")
    spacing = max(1, devices // 32)
    panels = devices // spacing
    slot_index = lax.axis_index("panel")
    panel_index = slot_index // spacing
    group_index = slot_index % spacing
    members = [[g + spacing * i for i in range(panels)] for g in range(spacing)]
    gather = functools.partial(
        lax.all_gather, axis_name="panel", axis_index_groups=members if spacing > 1 else None
    )
    blocks_here, snp_rows, panel_width = zscores.shape[1:]
    counts = lax.dynamic_slice_in_dim(eig_count, group_index * blocks_here, blocks_here)
    snps = lax.dynamic_slice_in_dim(snp_count, group_index * blocks_here, blocks_here)
    offsets = (jnp.cumsum(counts) - counts).astype(jnp.int32)
    row_total = panels * eig_vectors.shape[0]
    slab = min(row_total, KMAX + ALIGN)
    starts = jnp.minimum(offsets // ALIGN * ALIGN, row_total - slab)
    rounds = jnp.arange(ROUNDS + 1, dtype=jnp.int32)
    partners = (panel_index - rounds) % panels
    scales = samples.astype(jnp.float32).reshape(panels, panel_width)
    own_scale = lax.dynamic_index_in_dim(scales, panel_index, 0, keepdims=False)
    scale = 1.0 / jnp.sqrt(own_scale[None, :, None] * scales[partners][:, None, :])

    vectors = gather(eig_vectors, tiled=True)
    values = gather(eig_values, tiled=True)
    projected = project(vectors, zscores, starts, offsets, counts, snps)
    held = gather(projected)
    weighted = (projected.astype(jnp.float32) / values.astype(jnp.float32)[:, None]).astype(
        jnp.bfloat16
    )
    return grams(weighted, held, scale, partners, starts, offsets, counts)


def solution(mesh):
    placed = (
        P(("groups", "panel"), None),
        P(("groups", "panel")),
        P("groups"),
        P("groups"),
        P(("groups", "panel"), None, None, None),
        P("groups"),
    )
    return jax.shard_map(
        per_device,
        mesh=mesh,
        in_specs=placed,
        out_specs=P(None, ("groups", "panel"), None, None, None),
        check_vma=False,
    )
```

time: 812 us -> 183 us (0.23)
  loops' own time: 299 us -> 0 us
  local copies, waits for them, and re-layouts: 192 us -> 1.41 us
  matrix products: 105 us -> 0 us
  other arithmetic: 58.6 us -> 5.91 us
  blocking collectives: 0 us -> 31.7 us
  starting transfers between devices: 27.3 us -> 0.04 us
  Pallas kernels: 0 us -> 20.9 us
  between operations: 0.35 us -> 14 us
  waiting for transfers between devices: 121 us -> 108 us
    another operation x11 -> x0, loops' own time: 299 us -> none  [the longest x9 284 us: cross(): return lax.map(block_gram, jnp.arange(blocks_here, dtype=jnp.int32))]
    dynamic_slice x241 -> x0, local copies, waits for them, and re-layouts: 150 us -> none  [the longest x72 45.6 us: block_gram(): start_row = offsets[block_index]]
    ppermute x38 -> x0, waiting for transfers between devices: 121 us -> none  [passed_along(): lax.ppermute(shard, axis, [(i, (i + by) % size) for i in range(size)])]
    all_gather x0 -> x2, waiting for transfers between devices: none -> 108 us  [the longest x1 58.5 us: per_device(): vectors = gather(eig_vectors, tiled=True)]
    dot_general x80 -> x0, matrix products: 105 us -> none  [the longest x72 90.3 us: block_gram(): lax.dot_general(left_slab, right_slab, (((0,), (0,)), ((), ())), preferre...]
    and x80 -> x0, other arithmetic: 51.1 us -> none  [the longest x72 46.5 us: block_gram(): (row_index >= start_row) & (row_index < start_row + counts[block_index])]
    unnamed x0 -> x1, blocking collectives: none -> 31.7 us
    ppermute x38 -> x0, starting transfers between devices: 27.3 us -> none  [passed_along(): lax.ppermute(shard, axis, [(i, (i + by) % size) for i in range(size)])]
  transfers between devices with their start and end apart: 38 -> 2, of which waited for: 15 -> 2; matrix products, arithmetic and copies ran while one was open for 30% -> 4% of each run, Pallas kernels for 0% -> 0%
where the time goes in v1:
time: 183 us; the launch traced here: 182 us
  waiting for transfers between devices  108 us (59%)
  blocking collectives  31.7 us (17%)
  Pallas kernels  20.9 us (11%)
  between operations  14 us (8%)
  other arithmetic  5.91 us (3%)
    all_gather x1, waiting for transfers between devices, per_device(): vectors = gather(eig_vectors, tiled=True)  58.5 us
    all_gather x1, waiting for transfers between devices, per_device(): held = gather(projected)  49.2 us
    unnamed x1, blocking collectives  31.7 us
    pallas_call x1, Pallas kernels, grams(): pl.pallas_call(gram_kernel, out_shape=jax.ShapeDtypeStruct((rounds, 1, bl...  11.4 us
    pallas_call x1, Pallas kernels, project(): pl.pallas_call(project_kernel, out_shape=jax.ShapeDtypeStruct((row_total,...  9.47 us
  transfers between devices with their start and end apart: 2, of which 2 were waited for; matrix products, arithmetic and copies ran while one was open for 4% of the time, Pallas kernels for 0%

profile of v1, /device:TPU:1, one launch (start us, length us, event | category | flops | bytes accessed | tf_op | source)
XLA Modules:
  0.0 182.4 jit_solution(13171732345628899924)
XLA Ops:
  6.5 0.0 all-gather.4.cloned.1.call-start
  6.5 0.7 all-gather.4.cloned.1.call-update
  7.3 0.0 all-gather.6.cloned.1.call-start
  7.3 0.8 reduce-window.9
  8.1 1.2 multiply_minimum_fusion
  9.3 58.5 %all-gather.4.cloned.1.call-done.vectors = bf16[2560,1024]{1,0:T(8,128)(2,1)} async-done(((bf16[160,1024]{1,0:T(8,128)(2,1)}), bf16[2560,1024]{1,0:T(8,128)(2,1)}) %all-gather.4.cloned.1.call-update) | async-done | bytes 5242896 | tf_op jit(solution)/shard_map/all_gather | solution.py:117
  67.9 0.0 copy-start.2
  67.9 0.0 copy-start.1
  67.9 0.0 copy-start
  67.9 9.5 %shard_map.64 = bf16[2560,128]{1,0:T(8,128)(2,1)} custom-call(s32[8]{0:T(128)} %get-tuple-element.5.starts, s32[8]{0:T(128)} %get-tuple-element.6.offsets, s32[8]{0:T(128)} %counts.1, s32[8]{0:T(128)} %snps, bf16[2560,1024]{1,0:T(8,128)(2,1)} %all-gather.4.cloned.1.call-done.vectors, bf16[1,8,1024,128]{3,2,1,0:T(8,128)(2,1)} %scores.1), custom_call_target="tpu_custom_call" | custom-call | tf_op jit(solution)/shard_map/pallas_call | solution.py:34
  77.3 0.0 all-gather.6.cloned.1.call-update
  77.4 0.0 copy-done.2
  77.4 0.6 dynamic-slice
  78.5 0.0 copy-done.1
  78.5 0.2 dynamic-update-slice
  78.8 31.7 %all-reduce = bf16[2560]{0:T(1024)(128)(2,1)S(1)} all-reduce(bf16[2560]{0:T(1024)(128)(2,1)S(1)} %dynamic-update-slice), channel_id=1, replica_groups=mesh['groups'=2,'panel'=16] {'panel'}, use_global_device_ids=true, to_apply=%add | all-reduce | flops 2560 | bytes 10240
  110.5 0.0 copy-done
  110.5 0.6 gather_fusion
  111.1 0.5 and_select_fusion.1.slots
  111.6 1.0 multiply_rsqrt_fusion.scale
  112.6 2.4 %divide_convert_fusion.weighted = bf16[2560,128]{1,0:T(8,128)(2,1)} fusion(bf16[2560,128]{1,0:T(8,128)(2,1)} %shard_map.64, f32[2560]{0:T(1024)S(1)} %convert_element_type.11), kind=kLoop, calls=%fused_computation.1 | loop fusion | flops 983040 | bytes 1320960 | tf_op jit(solution)/shard_map/convert_element_type | solution.py:121
  114.9 49.2 %all-gather.6.cloned.1.call-done = bf16[40960,128]{1,0:T(8,128)(2,1)} async-done(((bf16[2560,128]{1,0:T(8,128)(2,1)}), bf16[40960,128]{1,0:T(8,128)(2,1)}) %all-gather.6.cloned.1.call-update) | async-done | bytes 10485776 | tf_op jit(solution)/shard_map/all_gather | solution.py:120
  164.2 11.4 %shard_map.65 = f32[9,1,8,128,128]{4,3,2,1,0:T(8,128)} custom-call(s32[8]{0:T(128)} %get-tuple-element.5.starts, s32[8]{0:T(128)} %get-tuple-element.6.offsets, s32[8]{0:T(128)} %counts.1, s32[9]{0:T(128)} %and_select_fusion.1.slots, bf16[2560,128]{1,0:T(8,128)(2,1)} %divide_convert_fusion.weighted, bf16[16,2560,128]{2,1,0:T(8,128)(2,1)} %bitcast.13, ...), custom_call_target="tpu_custom_call" | custom-call | tf_op jit(solution)/shard_map/pallas_call | solution.py:76
  (6 shorter events, 0.0 us)
Async XLA Ops:
  6.5 61.3 %all-gather.4.cloned.1.call-start = ((), (), s32[]{:S(2)}) async-start(), calls=%async_computation | async-start | bytes 5570560 | tf_op jit(solution)/shard_map/all_gather | solution.py:117
  7.3 156.9 %all-gather.6.cloned.1.call-start = ((), (), s32[]{:S(2)}) async-start(), calls=%async_computation.1 | async-start | bytes 11141120 | tf_op jit(solution)/shard_map/all_gather | solution.py:120
  67.9 9.5 %copy-start.2 = (u32[32]{0:T(128)S(1)}, u32[32]{0:T(128)}, u32[]{:S(2)}) copy-start(u32[32]{0:T(128)} %constant.70) | copy-start | bytes 388
  67.9 10.7 %copy-start.1 = (bf16[160]{0:T(256)(128)(2,1)S(1)}, bf16[160]{0:T(256)(128)(2,1)}, u32[]{:S(2)}) copy-start(bf16[160]{0:T(256)(128)(2,1)} %param.7) | copy-start | bytes 964
  67.9 42.6 %copy-start = (bf16[2048]{0:T(1024)(128)(2,1)S(1)}, bf16[2048]{0:T(1024)(128)(2,1)}, u32[]{:S(2)}) copy-start(bf16[2048]{0:T(1024)(128)(2,1)} %param.11) | copy-start | bytes 12292
Sparse Core Ops, SparseCore 0:
  9.6 58.2 all-gather.3
  77.5 86.6 all-gather.5

commit v2 on v1

v2 whole, which is shorter than its diff:
```python
import functools

import jax
import jax.numpy as jnp
from jax import lax
from jax.experimental import pallas as pl
from jax.experimental.pallas import tpu as pltpu
from jax.sharding import PartitionSpec as P

ROUNDS = 8
LIMIT = 56 * 1024 * 1024


def place_masked(snps, scores, pair, store):
    width = scores.shape[-1]
    for side in range(2):
        block = 2 * pair + side
        rows = lax.broadcasted_iota(jnp.int32, scores.shape[-2:], 0)
        part = jnp.where(rows < snps[block], scores[side].astype(jnp.float32), 0.0)
        store[:, side * width : (side + 1) * width] = part.astype(jnp.bfloat16)


def project_rows(vectors, masked, first_count):
    both = jnp.dot(vectors, masked, preferred_element_type=jnp.float32)
    width = both.shape[1] // 2
    rows = lax.broadcasted_iota(jnp.int32, (both.shape[0], width), 0)
    return jnp.where(rows < first_count, both[:, :width], both[:, width:]).astype(jnp.bfloat16)


def project_kernel(counts, snps, vectors, scores, out, masked):
    pair = pl.program_id(0)
    place_masked(snps, scores.at[0], pair, masked)
    out[...] = project_rows(vectors[...], masked[...], counts[2 * pair])


def project(vectors, scores, counts, snps):
    row_total, depth = vectors.shape
    blocks, snp_rows, width = scores.shape[1:]
    pair_rows = 2 * row_total // blocks
    return pl.pallas_call(
        project_kernel,
        out_shape=jax.ShapeDtypeStruct((row_total, width), jnp.bfloat16),
        grid_spec=pltpu.PrefetchScalarGridSpec(
            num_scalar_prefetch=2,
            grid=(blocks // 2,),
            in_specs=[
                pl.BlockSpec((pair_rows, depth), lambda b, *_: (b, 0)),
                pl.BlockSpec((1, 2, snp_rows, width), lambda b, *_: (0, b, 0, 0)),
            ],
            out_specs=pl.BlockSpec((pair_rows, width), lambda b, *_: (b, 0)),
            scratch_shapes=[pltpu.VMEM((snp_rows, 2 * width), jnp.bfloat16)],
        ),
        compiler_params=pltpu.CompilerParams(vmem_limit_bytes=LIMIT),
    )(counts, snps, vectors, scores)


def gram_kernel(counts, slots, weighted, panels, scale, out):
    pair = pl.program_id(0)
    width = weighted.shape[1]
    left = weighted[...].astype(jnp.float32)
    rows = lax.broadcasted_iota(jnp.int32, left.shape, 0)
    first = rows < counts[2 * pair]
    left = jnp.concatenate([jnp.where(first, left, 0.0).T, jnp.where(first, 0.0, left).T], axis=0)
    left = left.astype(jnp.bfloat16)
    shape = (width, width)
    same = lax.broadcasted_iota(jnp.int32, shape, 0) == lax.broadcasted_iota(jnp.int32, shape, 1)
    for index in range(out.shape[0]):
        both = jnp.dot(left, panels[slots[index]], preferred_element_type=jnp.float32)
        for side in range(2):
            gram = both[side * width : (side + 1) * width]
            if index == 0:
                count = counts[2 * pair + side].astype(jnp.float32)
                gram = gram - jnp.where(same, count, 0.0)
            out[index, 0, side] = gram * scale[index]


def grams(weighted, panels, scale, slots, counts):
    blocks = counts.shape[0]
    rounds, width = scale.shape[:2]
    pair_rows = 2 * weighted.shape[0] // blocks
    return pl.pallas_call(
        gram_kernel,
        out_shape=jax.ShapeDtypeStruct((rounds, 1, blocks, width, width), jnp.float32),
        grid_spec=pltpu.PrefetchScalarGridSpec(
            num_scalar_prefetch=2,
            grid=(blocks // 2,),
            in_specs=[
                pl.BlockSpec((pair_rows, width), lambda b, *_: (b, 0)),
                pl.BlockSpec((panels.shape[0], pair_rows, width), lambda b, *_: (0, b, 0)),
                pl.BlockSpec(scale.shape, lambda b, *_: (0, 0, 0)),
            ],
            out_specs=pl.BlockSpec((rounds, 1, 2, width, width), lambda b, *_: (0, 0, b, 0, 0)),
        ),
        compiler_params=pltpu.CompilerParams(vmem_limit_bytes=LIMIT),
    )(counts, slots, weighted, panels, scale)


def exchange_kernel(counts, snps, own, own_values, scores, held, values, store, masked, here,
                    send1, recv1, send2, recv2, send3, recv3):
    line = lax.axis_size("panel") // 4
    me = lax.axis_index("panel")
    z = me // 4
    y = (me // 2) % 2
    k = me % 2
    piece = own.shape[0]
    pair_rows = 4 * piece
    halves = recv1.shape[1]
    part = piece // halves
    chunks = recv2.shape[1]
    top = line - 1
    up, down, across, beside = me + 4, me - 4, me + 2 - 4 * y, me + 1 - 2 * k
    pending = []

    barrier = pltpu.get_barrier_semaphore()
    others = 4 * line - 1
    for step in range(1, others + 1):
        target = lax.rem(me + step, others + 1)
        pl.semaphore_signal(
            barrier, inc=1, device_id={"panel": target}, device_id_type=pl.DeviceIdType.MESH
        )
    pl.semaphore_wait(barrier, others)

    def start(condition, copy):
        if condition is None:
            copy.start()
        else:
            pl.when(condition)(copy.start)
        pending.append((condition, copy))

    def move1(source, half, way, target, first=False):
        rows = pl.ds(source * piece + half * part, part)
        origin = own.at[pl.ds(half * part, part)] if first else store.at[rows]
        return pltpu.make_async_remote_copy(
            src_ref=origin,
            dst_ref=store.at[rows],
            send_sem=send1.at[way, source, half],
            recv_sem=recv1.at[source, half],
            device_id={"panel": target},
            device_id_type=pl.DeviceIdType.MESH,
        )

    def arrive1(source, half):
        move1(source, half, 0, beside).wait_recv()

    def move2(source, chunk, way, target):
        rows = pl.ds(chunk * pair_rows, pair_rows)
        return pltpu.make_async_remote_copy(
            src_ref=held.at[source, rows],
            dst_ref=held.at[source, rows],
            send_sem=send2.at[way, source, chunk],
            recv_sem=recv2.at[source, chunk],
            device_id={"panel": target},
            device_id_type=pl.DeviceIdType.MESH,
        )

    def arrive2(source, chunk):
        move2(source, chunk, 0, beside).wait_recv()

    def move3(source, step, target):
        return pltpu.make_async_remote_copy(
            src_ref=own_values,
            dst_ref=values.at[source],
            send_sem=send3.at[step],
            recv_sem=recv3.at[source],
            device_id={"panel": target},
            device_id_type=pl.DeviceIdType.MESH,
        )

    for half in range(halves):
        start(z < top, move1(me, half, 0, up, True))
        start(z > 0, move1(me, half, 1, down, True))
        start(None, move1(me, half, 2, across, True))
        start(None, move1(me, half, 3, beside, True))
    for step in range(1, others + 1):
        start(None, move3(me, step, lax.rem(me + step, others + 1)))
    local = [
        pltpu.make_async_copy(own, store.at[pl.ds(me * piece, piece)], here.at[0]),
        pltpu.make_async_copy(own_values, values.at[me], here.at[1]),
    ]
    for copy in local:
        copy.start()
    for pair in range(line):
        place_masked(snps, scores.at[0, pl.ds(2 * pair, 2)], pair, masked.at[pair])
    for copy in local:
        copy.wait()

    def plane(index):
        rows = pl.ds(index * pair_rows, pair_rows)
        held[me, rows] = project_rows(store[rows], masked[index], counts[2 * index])

    def column(distance):
        for half in range(halves):
            def below():
                arrive1(me - 4 * distance, half)
            def above():
                arrive1(me + 4 * distance, half)
            has_below, has_above = z >= distance, z + distance <= top
            pl.when(has_below)(below)
            source = me - 4 * distance
            start(has_below & (z < top), move1(source, half, 0, up))
            start(has_below, move1(source, half, 2, across))
            start(has_below, move1(source, half, 3, beside))
            pl.when(has_above)(above)
            source = me + 4 * distance
            start(has_above & (z > 0), move1(source, half, 1, down))
            start(has_above, move1(source, half, 2, across))
            start(has_above, move1(source, half, 3, beside))

    def sideways(distance, sign):
        has = (z >= distance) if sign < 0 else (z + distance <= top)
        source = across + sign * 4 * distance
        for half in range(halves):
            pl.when(has)(functools.partial(arrive1, source, half))
            start(has, move1(source, half, 3, beside))

    def finish(distance, sign):
        has = (z >= distance) if sign < 0 else (z + distance <= top)

        @pl.when(has)
        def _():
            for source in (beside, beside + 2 - 4 * y):
                for half in range(halves):
                    arrive1(source + sign * 4 * distance, half)
            plane(z + sign * distance)

    for distance in range(1, line + 1):
        if distance < line:
            column(distance)
        last = distance - 1
        signs = (1,) if last == 0 else (-1, 1)
        for sign in signs:
            sideways(last, sign)
        for sign in signs:
            finish(last, sign)

    def spread(condition, chunk, source, behind):
        side = (behind >= y) & (behind <= y + 1)
        near = behind <= 2
        start(condition & side, move2(source, chunk, 2, across))
        start(condition & near, move2(source, chunk, 3, beside))

    always = me >= 0
    cross = []
    for lag in range(2):
        plane_index = lax.rem(z - lag - (1 - y) + line, line)
        cross.append(plane_index * 4 + (1 - y) * 2 + k)
    for chunk in range(chunks):
        start(z < top, move2(me, chunk, 0, up))
        start(z >= line - 2, move2(me, chunk, 1, down))
        spread(always, chunk, me, 0)
    for chunk in range(chunks + 1):
        if chunk < chunks:
            for distance in range(1, line):
                if distance <= 2:
                    has = z >= distance
                    source = me - 4 * distance
                    pl.when(has)(functools.partial(arrive2, source, chunk))
                    if distance == 1:
                        start(has & (z < top), move2(source, chunk, 0, up))
                    spread(has, chunk, source, distance)
                has = (z + distance <= top) & (z + distance >= line - 2)
                source = me + 4 * distance
                pl.when(has)(functools.partial(arrive2, source, chunk))
                start(has & (z > 0), move2(source, chunk, 1, down))
                spread(has, chunk, source, line - distance)
        if chunk > 0:
            for source in cross:
                arrive2(source, chunk - 1)
                start(None, move2(source, chunk - 1, 3, beside))
    for chunk in range(chunks):
        for source in cross:
            arrive2(source + 1 - 2 * k, chunk)
        for behind in range(3):
            plane_index = lax.rem(z - behind + line, line)
            arrive2(plane_index * 4 + y * 2 + 1 - k, chunk)
    for step in range(1, others + 1):
        move3(lax.rem(me + step, others + 1), step, beside).wait_recv()
    for condition, copy in pending:
        if condition is None:
            copy.wait_send()
        else:
            pl.when(condition)(copy.wait_send)


def exchange(vectors, values, counts, snps, scores):
    devices = lax.axis_size("panel")
    piece, depth = vectors.shape
    blocks, snp_rows, width = scores.shape[1:]
    row_total = devices * piece
    lanes = -(-piece // 128) * 128
    rider = jnp.pad(values.astype(jnp.float32), (0, lanes - piece))
    rider = jnp.broadcast_to(rider, (8, lanes))
    halves = 2
    chunks = blocks // 2
    vmem = pl.BlockSpec(memory_space=pltpu.VMEM)
    smem = pl.BlockSpec(memory_space=pltpu.SMEM)
    held, gathered = pl.pallas_call(
        exchange_kernel,
        out_shape=(
            jax.ShapeDtypeStruct((devices, row_total, width), jnp.bfloat16),
            jax.ShapeDtypeStruct((devices, 8, lanes), jnp.float32),
        ),
        in_specs=[smem, smem, vmem, vmem, vmem],
        out_specs=(vmem, vmem),
        scratch_shapes=[
            pltpu.VMEM((row_total, depth), jnp.bfloat16),
            pltpu.VMEM((blocks // 2, snp_rows, 2 * width), jnp.bfloat16),
            pltpu.SemaphoreType.DMA((2,)),
            pltpu.SemaphoreType.DMA((4, devices, halves)),
            pltpu.SemaphoreType.DMA((devices, halves)),
            pltpu.SemaphoreType.DMA((4, devices, chunks)),
            pltpu.SemaphoreType.DMA((devices, chunks)),
            pltpu.SemaphoreType.DMA((devices,)),
            pltpu.SemaphoreType.DMA((devices,)),
        ],
        compiler_params=pltpu.CompilerParams(
            collective_id=0, has_side_effects=True, vmem_limit_bytes=LIMIT
        ),
    )(counts, snps, vectors, rider, scores)
    return held, gathered[:, 0, :piece].reshape(-1)


def per_device(eig_vectors, eig_values, eig_count, snp_count, zscores, samples):
    devices = lax.axis_size("panel")
    spacing = max(1, devices // 32)
    panels = devices // spacing
    slot_index = lax.axis_index("panel")
    panel_index = slot_index // spacing
    group_index = slot_index % spacing
    blocks_here, snp_rows, panel_width = zscores.shape[1:]
    counts = lax.dynamic_slice_in_dim(eig_count, group_index * blocks_here, blocks_here)
    snps = lax.dynamic_slice_in_dim(snp_count, group_index * blocks_here, blocks_here)
    rounds = jnp.arange(ROUNDS + 1, dtype=jnp.int32)
    partners = (panel_index - rounds) % panels
    scales = samples.astype(jnp.float32).reshape(panels, panel_width)
    own_scale = lax.dynamic_index_in_dim(scales, panel_index, 0, keepdims=False)
    scale = 1.0 / jnp.sqrt(own_scale[None, :, None] * scales[partners][:, None, :])

    if spacing == 1 and panels == 2 * ROUNDS and blocks_here == panels // 2:
        held, values = exchange(eig_vectors, eig_values, counts, snps, zscores)
        projected = lax.dynamic_index_in_dim(held, panel_index, 0, keepdims=False)
    else:
        members = [[g + spacing * i for i in range(panels)] for g in range(spacing)]
        gather = functools.partial(
            lax.all_gather, axis_name="panel", axis_index_groups=members if spacing > 1 else None
        )
        vectors = gather(eig_vectors, tiled=True)
        values = gather(eig_values, tiled=True)
        projected = project(vectors, zscores, counts, snps)
        held = gather(projected)
    weighted = (projected.astype(jnp.float32) / values.astype(jnp.float32)[:, None]).astype(
        jnp.bfloat16
    )
    return grams(weighted, held, scale, partners, counts)


def solution(mesh):
    placed = (
        P(("groups", "panel"), None),
        P(("groups", "panel")),
        P("groups"),
        P("groups"),
        P(("groups", "panel"), None, None, None),
        P("groups"),
    )
    return jax.shard_map(
        per_device,
        mesh=mesh,
        in_specs=placed,
        out_specs=P(None, ("groups", "panel"), None, None, None),
        check_vma=False,
    )
```

time: 183 us -> 118 us (0.64)
  waiting for transfers between devices: 108 us -> 0 us
  Pallas kernels: 20.9 us -> 110 us
  blocking collectives: 31.7 us -> 0 us
  between operations: 14 us -> 0.02 us
    all_gather x2 -> x0, waiting for transfers between devices: 108 us -> none  [the longest x1 58.5 us: per_device(): vectors = gather(eig_vectors, tiled=True)]
    pallas_call x1, Pallas kernels: 9.47 us -> 101 us  [exchange(): pl.pallas_call(exchange_kernel, out_shape=(jax.ShapeDtypeStruct((devices,...]
    unnamed x1 -> x0, blocking collectives: 31.7 us -> none
    pallas_call x1, Pallas kernels: 11.4 us -> 9.37 us  [grams(): pl.pallas_call(gram_kernel, out_shape=jax.ShapeDtypeStruct((rounds, 1, bl...]
  transfers between devices with their start and end apart: 2 -> 0, of which waited for: 2 -> 0; matrix products, arithmetic and copies ran while one was open for 4% -> 0% of each run, Pallas kernels for 0% -> 0%
where the time goes in v2:
time: 118 us
  Pallas kernels  110 us (93%)
  other arithmetic  5.31 us (4%)
  local copies, waits for them, and re-layouts  2.18 us (2%)
    pallas_call x1, Pallas kernels, exchange(): pl.pallas_call(exchange_kernel, out_shape=(jax.ShapeDtypeStruct((devices,...  101 us
    pallas_call x1, Pallas kernels, grams(): pl.pallas_call(gram_kernel, out_shape=jax.ShapeDtypeStruct((rounds, 1, bl...  9.37 us
    convert_element_type x1, other arithmetic, per_device(): (projected.astype(jnp.float32) / values.astype(jnp.float32)[:, None]).ast...  2.36 us

profile of v2, /device:TPU:1, one launch (start us, length us, event | category | flops | bytes accessed | tf_op | source)
XLA Modules:
  0.0 117.7 jit_solution(4968836936844821396)
XLA Ops:
  0.0 0.6 and_select_fusion.1.slots
  0.6 0.7 pad_convert_fusion
  1.3 0.6 broadcast_in_dim.2.own_values
  1.9 0.7 bitcast_convert_fusion
  2.6 0.6 gather_fusion
  3.1 1.0 multiply_rsqrt_fusion.scale
  4.1 100.8 %shard_map.64 = (bf16[16,2560,128]{2,1,0:T(8,128)(2,1)}, f32[16,8,256]{2,1,0:T(8,128)}) custom-call(s32[8]{0:T(128)} %counts.1, s32[8]{0:T(128)} %snps, bf16[160,1024]{1,0:T(8,128)(2,1)} %own.1, f32[8,256]{1,0:T(8,128)} %broadcast_in_dim.2.own_values, bf16[1,8,1024,128]{3,2,1,0:T(8,128)(2,1)} %scores.1), custom_call_target="tpu_custom_call" | custom-call | tf_op jit(solution)/shard_map/pallas_call | solution.py:297
  104.9 0.9 slice_reduce_fusion
  105.9 0.1 div.14
  105.9 2.4 %fusion.weighted = bf16[2560,128]{1,0:T(8,128)(2,1)} fusion(f32[2560]{0:T(1024)S(1)} %div.14, bf16[16,2560,128]{2,1,0:T(8,128)(2,1)} %get-tuple-element.7.panels, s32[]{:T(128)S(6)} %select_n.34), kind=kLoop, calls=%fused_computation.2 | loop fusion | flops 983040 | bytes 1320964 | tf_op jit(solution)/shard_map/convert_element_type | solution.py:351
  108.3 9.4 %shard_map.65 = f32[9,1,8,128,128]{4,3,2,1,0:T(8,128)} custom-call(s32[8]{0:T(128)} %counts.1, s32[9]{0:T(128)} %and_select_fusion.1.slots, bf16[2560,128]{1,0:T(8,128)(2,1)} %fusion.weighted, bf16[16,2560,128]{2,1,0:T(8,128)(2,1)} %get-tuple-element.7.panels, f32[9,128,128]{2,1,0:T(8,128)} %multiply_rsqrt_fusion.scale), custom_call_target="tpu_custom_call" | custom-call | tf_op jit(solution)/shard_map/pallas_call | solution.py:81
  (3 shorter events, 0.0 us)

commit v3 on v2

--- a/solution.py
+++ b/solution.py
@@ -166,6 +166,18 @@
             device_id_type=pl.DeviceIdType.MESH,
         )
 
+    def spread(condition, chunk, source, behind):
+        side = (behind >= y) & (behind <= y + 1)
+        near = behind <= 2
+        start(condition & side, move2(source, chunk, 2, across))
+        start(condition & near, move2(source, chunk, 3, beside))
+
+    def order(source, step):
+        far = source // 4
+        near = jnp.minimum(far, top - far)
+        nearest = jnp.where(step > 2 * near, step, (near + (step + 1) // 2 * (1 - 2 * (step % 2))))
+        return jnp.where(far > top - far, top - nearest, nearest)
+
     for half in range(halves):
         start(z < top, move1(me, half, 0, up, True))
         start(z > 0, move1(me, half, 1, down, True))
@@ -223,6 +235,11 @@
                     arrive1(source + sign * 4 * distance, half)
             plane(z + sign * distance)
 
+        chunk = z + sign * distance
+        start(has & (z < top), move2(me, chunk, 0, up))
+        start(has & (z >= line - 2), move2(me, chunk, 1, down))
+        spread(has, chunk, me, 0)
+
     for distance in range(1, line + 1):
         if distance < line:
             column(distance)
@@ -233,40 +250,32 @@
         for sign in signs:
             finish(last, sign)
 
-    def spread(condition, chunk, source, behind):
-        side = (behind >= y) & (behind <= y + 1)
-        near = behind <= 2
-        start(condition & side, move2(source, chunk, 2, across))
-        start(condition & near, move2(source, chunk, 3, beside))
-
-    always = me >= 0
     cross = []
     for lag in range(2):
         plane_index = lax.rem(z - lag - (1 - y) + line, line)
         cross.append(plane_index * 4 + (1 - y) * 2 + k)
-    for chunk in range(chunks):
-        start(z < top, move2(me, chunk, 0, up))
-        start(z >= line - 2, move2(me, chunk, 1, down))
-        spread(always, chunk, me, 0)
-    for chunk in range(chunks + 1):
-        if chunk < chunks:
+    for step in range(chunks + 1):
+        if step < chunks:
             for distance in range(1, line):
                 if distance <= 2:
                     has = z >= distance
                     source = me - 4 * distance
+                    chunk = order(source, step)
                     pl.when(has)(functools.partial(arrive2, source, chunk))
                     if distance == 1:
                         start(has & (z < top), move2(source, chunk, 0, up))
                     spread(has, chunk, source, distance)
                 has = (z + distance <= top) & (z + distance >= line - 2)
                 source = me + 4 * distance
+                chunk = order(source, step)
                 pl.when(has)(functools.partial(arrive2, source, chunk))
                 start(has & (z > 0), move2(source, chunk, 1, down))
                 spread(has, chunk, source, line - distance)
-        if chunk > 0:
+        if step > 0:
             for source in cross:
-                arrive2(source, chunk - 1)
-                start(None, move2(source, chunk - 1, 3, beside))
+                chunk = order(source, step - 1)
+                arrive2(source, chunk)
+                start(None, move2(source, chunk, 3, beside))
     for chunk in range(chunks):
         for source in cross:
             arrive2(source + 1 - 2 * k, chunk)

time: 118 us -> 112 us (0.949)
  Pallas kernels: 110 us -> 104 us
    pallas_call x1, Pallas kernels: 101 us -> 94.8 us  [exchange(): pl.pallas_call(exchange_kernel, out_shape=(jax.ShapeDtypeStruct((devices,...]
where the time goes in v3:
time: 112 us
  Pallas kernels  104 us (93%)
  other arithmetic  5.31 us (5%)
  local copies, waits for them, and re-layouts  2.18 us (2%)
    pallas_call x1, Pallas kernels, exchange(): pl.pallas_call(exchange_kernel, out_shape=(jax.ShapeDtypeStruct((devices,...  94.8 us
    pallas_call x1, Pallas kernels, grams(): pl.pallas_call(gram_kernel, out_shape=jax.ShapeDtypeStruct((rounds, 1, bl...  9.37 us
    convert_element_type x1, other arithmetic, per_device(): (projected.astype(jnp.float32) / values.astype(jnp.float32)[:, None]).ast...  2.36 us

profile of v3, /device:TPU:1, one launch (start us, length us, event | category | flops | bytes accessed | tf_op | source)
XLA Modules:
  0.0 111.7 jit_solution(5298018283502508142)
XLA Ops:
  0.0 0.6 and_select_fusion.1.slots
  0.6 0.7 pad_convert_fusion
  1.3 0.6 broadcast_in_dim.2.own_values
  1.9 0.7 bitcast_convert_fusion
  2.6 0.6 gather_fusion
  3.1 1.0 multiply_rsqrt_fusion.scale
  4.1 94.8 %shard_map.64 = (bf16[16,2560,128]{2,1,0:T(8,128)(2,1)}, f32[16,8,256]{2,1,0:T(8,128)}) custom-call(s32[8]{0:T(128)} %counts.1, s32[8]{0:T(128)} %snps, bf16[160,1024]{1,0:T(8,128)(2,1)} %own.1, f32[8,256]{1,0:T(8,128)} %broadcast_in_dim.2.own_values, bf16[1,8,1024,128]{3,2,1,0:T(8,128)(2,1)} %scores.1), custom_call_target="tpu_custom_call" | custom-call | tf_op jit(solution)/shard_map/pallas_call | solution.py:306
  98.9 0.9 slice_reduce_fusion
  99.9 0.1 div.14
  99.9 2.4 %fusion.weighted = bf16[2560,128]{1,0:T(8,128)(2,1)} fusion(f32[2560]{0:T(1024)S(1)} %div.14, bf16[16,2560,128]{2,1,0:T(8,128)(2,1)} %get-tuple-element.7.panels, s32[]{:T(128)S(6)} %select_n.34), kind=kLoop, calls=%fused_computation.2 | loop fusion | flops 983040 | bytes 1320964 | tf_op jit(solution)/shard_map/convert_element_type | solution.py:360
  102.3 9.4 %shard_map.65 = f32[9,1,8,128,128]{4,3,2,1,0:T(8,128)} custom-call(s32[8]{0:T(128)} %counts.1, s32[9]{0:T(128)} %and_select_fusion.1.slots, bf16[2560,128]{1,0:T(8,128)(2,1)} %fusion.weighted, bf16[16,2560,128]{2,1,0:T(8,128)(2,1)} %get-tuple-element.7.panels, f32[9,128,128]{2,1,0:T(8,128)} %multiply_rsqrt_fusion.scale), custom_call_target="tpu_custom_call" | custom-call | tf_op jit(solution)/shard_map/pallas_call | solution.py:81
  (3 shorter events, 0.0 us)

commit v4 on v3

--- a/solution.py
+++ b/solution.py
@@ -95,8 +95,8 @@
     )(counts, slots, weighted, panels, scale)
 
 
-def exchange_kernel(counts, snps, own, own_values, scores, held, values, store, masked, here,
-                    send1, recv1, send2, recv2, send3, recv3):
+def exchange_kernel(counts, snps, own, own_values, scores, out, held, values, left, store, masked,
+                    here, send1, recv1, send2, recv2, send3, recv3):
     line = lax.axis_size("panel") // 4
     me = lax.axis_index("panel")
     z = me // 4
@@ -254,7 +254,33 @@
     for lag in range(2):
         plane_index = lax.rem(z - lag - (1 - y) + line, line)
         cross.append(plane_index * 4 + (1 - y) * 2 + k)
-    for step in range(chunks + 1):
+    def weigh(index):
+        rows = pl.ds(index * pair_rows, pair_rows)
+        row = values[4 * index] + values[4 * index + 1]
+        row = row + (values[4 * index + 2] + values[4 * index + 3])
+        flat = held[me, rows].astype(jnp.float32).T / row[0:1]
+        first = lax.broadcasted_iota(jnp.int32, flat.shape, 1) < counts[2 * index]
+        both = jnp.concatenate([jnp.where(first, flat, 0.0), jnp.where(first, 0.0, flat)], axis=0)
+        left[index] = both.astype(jnp.bfloat16)
+
+    def gram(source, chunk, number, own_panel=False):
+        rows = pl.ds(chunk * pair_rows, pair_rows)
+        both = jnp.dot(left[chunk], held[source, rows], preferred_element_type=jnp.float32)
+        width = both.shape[1]
+        for side in range(2):
+            part = both[side * width : (side + 1) * width]
+            if own_panel:
+                shape = (width, width)
+                across_rows = lax.broadcasted_iota(jnp.int32, shape, 0)
+                same = across_rows == lax.broadcasted_iota(jnp.int32, shape, 1)
+                count = counts[2 * chunk + side].astype(jnp.float32)
+                part = part - jnp.where(same, count, 0.0)
+            out[number, 0, 2 * chunk + side] = part
+
+    near = [lax.rem(z - lag + line, line) * 4 + y * 2 + k for lag in range(3)]
+    swap = 1 - 2 * k
+
+    for step in range(chunks + 2):
         if step < chunks:
             for distance in range(1, line):
                 if distance <= 2:
@@ -271,19 +297,35 @@
                 pl.when(has)(functools.partial(arrive2, source, chunk))
                 start(has & (z > 0), move2(source, chunk, 1, down))
                 spread(has, chunk, source, line - distance)
-        if step > 0:
+        if step == 0:
+            for number in range(1, others + 1):
+                move3(lax.rem(me + number, others + 1), number, beside).wait_recv()
+            for index in range(chunks):
+                weigh(index)
+        if 0 < step <= chunks:
             for source in cross:
                 chunk = order(source, step - 1)
                 arrive2(source, chunk)
                 start(None, move2(source, chunk, 3, beside))
-    for chunk in range(chunks):
-        for source in cross:
-            arrive2(source + 1 - 2 * k, chunk)
-        for behind in range(3):
-            plane_index = lax.rem(z - behind + line, line)
-            arrive2(plane_index * 4 + y * 2 + 1 - k, chunk)
-    for step in range(1, others + 1):
-        move3(lax.rem(me + step, others + 1), step, beside).wait_recv()
+        if 0 < step <= chunks:
+            for lag, source in enumerate(near):
+                gram(source, order(source, step - 1), 4 * lag, lag == 0)
+            for lag, source in enumerate(cross):
+                gram(source, order(source, step - 1), 4 * lag + 2)
+        if step > 1:
+            for lag, source in enumerate(near):
+                chunk = order(source, step - 2)
+                arrive2(source + swap, chunk)
+                number = 4 * lag - swap
+
+                @pl.when((number >= 0) & (number < out.shape[0]))
+                def _():
+                    gram(source + swap, chunk, number)
+
+            for lag, source in enumerate(cross):
+                chunk = order(source, step - 2)
+                arrive2(source + swap, chunk)
+                gram(source + swap, chunk, 4 * lag + 2 - swap)
     for condition, copy in pending:
         if condition is None:
             copy.wait_send()
@@ -296,22 +338,24 @@
     piece, depth = vectors.shape
     blocks, snp_rows, width = scores.shape[1:]
     row_total = devices * piece
-    lanes = -(-piece // 128) * 128
-    rider = jnp.pad(values.astype(jnp.float32), (0, lanes - piece))
-    rider = jnp.broadcast_to(rider, (8, lanes))
+    pair_rows = 4 * piece
+    place = lax.rem(lax.axis_index("panel"), 4) * piece
+    rider = jnp.zeros((8, pair_rows), jnp.float32)
+    spread = jnp.broadcast_to(values.astype(jnp.float32), (8, piece))
+    rider = lax.dynamic_update_slice_in_dim(rider, spread, place, 1)
     halves = 2
     chunks = blocks // 2
     vmem = pl.BlockSpec(memory_space=pltpu.VMEM)
     smem = pl.BlockSpec(memory_space=pltpu.SMEM)
-    held, gathered = pl.pallas_call(
+    return pl.pallas_call(
         exchange_kernel,
-        out_shape=(
-            jax.ShapeDtypeStruct((devices, row_total, width), jnp.bfloat16),
-            jax.ShapeDtypeStruct((devices, 8, lanes), jnp.float32),
-        ),
+        out_shape=jax.ShapeDtypeStruct((ROUNDS + 1, 1, blocks, width, width), jnp.float32),
         in_specs=[smem, smem, vmem, vmem, vmem],
-        out_specs=(vmem, vmem),
+        out_specs=vmem,
         scratch_shapes=[
+            pltpu.VMEM((devices, row_total, width), jnp.bfloat16),
+            pltpu.VMEM((devices, 8, pair_rows), jnp.float32),
+            pltpu.VMEM((chunks, 2 * width, pair_rows), jnp.bfloat16),
             pltpu.VMEM((row_total, depth), jnp.bfloat16),
             pltpu.VMEM((blocks // 2, snp_rows, 2 * width), jnp.bfloat16),
             pltpu.SemaphoreType.DMA((2,)),
@@ -326,7 +370,6 @@
             collective_id=0, has_side_effects=True, vmem_limit_bytes=LIMIT
         ),
     )(counts, snps, vectors, rider, scores)
-    return held, gathered[:, 0, :piece].reshape(-1)
 
 
 def per_device(eig_vectors, eig_values, eig_count, snp_count, zscores, samples):
@@ -346,17 +389,16 @@
     scale = 1.0 / jnp.sqrt(own_scale[None, :, None] * scales[partners][:, None, :])
 
     if spacing == 1 and panels == 2 * ROUNDS and blocks_here == panels // 2:
-        held, values = exchange(eig_vectors, eig_values, counts, snps, zscores)
-        projected = lax.dynamic_index_in_dim(held, panel_index, 0, keepdims=False)
-    else:
-        members = [[g + spacing * i for i in range(panels)] for g in range(spacing)]
-        gather = functools.partial(
-            lax.all_gather, axis_name="panel", axis_index_groups=members if spacing > 1 else None
-        )
-        vectors = gather(eig_vectors, tiled=True)
-        values = gather(eig_values, tiled=True)
-        projected = project(vectors, zscores, counts, snps)
-        held = gather(projected)
+        raw = exchange(eig_vectors, eig_values, counts, snps, zscores)
+        return raw * scale[:, None, None]
+    members = [[g + spacing * i for i in range(panels)] for g in range(spacing)]
+    gather = functools.partial(
+        lax.all_gather, axis_name="panel", axis_index_groups=members if spacing > 1 else None
+    )
+    vectors = gather(eig_vectors, tiled=True)
+    values = gather(eig_values, tiled=True)
+    projected = project(vectors, zscores, counts, snps)
+    held = gather(projected)
     weighted = (projected.astype(jnp.float32) / values.astype(jnp.float32)[:, None]).astype(
         jnp.bfloat16
     )

time: 112 us -> 104 us (0.929)
  Pallas kernels: 104 us -> 95.6 us
    pallas_call x2 -> x1, Pallas kernels: 104 us -> 95.6 us  [exchange(): pl.pallas_call(exchange_kernel, out_shape=jax.ShapeDtypeStruct((ROUNDS +...]
    mul x0 -> x1, other arithmetic: none -> 5.43 us  [per_device(): return raw * scale[:, None, None]]
    convert_element_type x1 -> x0, other arithmetic: 2.36 us -> none  [per_device(): (projected.astype(jnp.float32) / values.astype(jnp.float32)[:, None]).ast...]
where the time goes in v4:
time: 104 us; the launch traced here: 103 us
  Pallas kernels  95.6 us (92%)
  other arithmetic  5.61 us (5%)
  local copies, waits for them, and re-layouts  2.11 us (2%)
    pallas_call x1, Pallas kernels, exchange(): pl.pallas_call(exchange_kernel, out_shape=jax.ShapeDtypeStruct((ROUNDS +...  95.6 us
    mul x1, other arithmetic, per_device(): return raw * scale[:, None, None]  5.43 us

profile of v4, /device:TPU:1, one launch (start us, length us, event | category | flops | bytes accessed | tf_op | source)
XLA Modules:
  0.0 103.4 jit_solution(7179943406357883581)
XLA Ops:
  0.0 0.0 copy-start.1
  0.0 0.7 broadcast_in_dim.5
  0.7 0.3 dynamic_update_slice.3.own_values
  0.9 0.0 copy-start
  0.9 0.6 copy-done
  1.5 95.6 %shard_map.64 = f32[9,1,8,128,128]{4,3,2,1,0:T(8,128)} custom-call(s32[8]{0:T(128)} %counts, s32[8]{0:T(128)} %snps, bf16[160,1024]{1,0:T(8,128)(2,1)} %own.1, f32[8,640]{1,0:T(8,128)} %copy-done, bf16[1,8,1024,128]{3,2,1,0:T(8,128)(2,1)} %scores.1), custom_call_target="tpu_custom_call" | custom-call | tf_op jit(solution)/shard_map/pallas_call | solution.py:350
  97.2 0.0 copy-done.1
  97.3 0.6 gather_fusion
  97.8 0.2 multiply_rsqrt_fusion
  98.0 5.4 %broadcast_multiply_fusion = f32[9,1,8,128,128]{4,3,2,1,0:T(8,128)} fusion(f32[9,1,8,128,128]{4,3,2,1,0:T(8,128)} %shard_map.64, f32[9,128,128]{2,1,0:T(8,128)S(1)} %multiply_rsqrt_fusion), kind=kLoop, calls=%fused_computation.1 | loop fusion | flops 1179648 | bytes 10027008 | tf_op jit(solution)/shard_map/mul | solution.py:393
  (5 shorter events, 0.0 us)
Async XLA Ops:
  0.0 97.2 %copy-start.1 = (bf16[2048]{0:T(1024)(128)(2,1)S(1)}, bf16[2048]{0:T(1024)(128)(2,1)}, u32[]{:S(2)}) copy-start(bf16[2048]{0:T(1024)(128)(2,1)} %param.11) | copy-start | bytes 12292
  0.9 0.6 copy-start

commit v5 on v4

--- a/solution.py
+++ b/solution.py
@@ -8,6 +8,8 @@
 from jax.sharding import PartitionSpec as P
 
 ROUNDS = 8
+HALVES = 5
+CUTS = 2
 LIMIT = 56 * 1024 * 1024
 
 
@@ -106,7 +108,10 @@
     pair_rows = 4 * piece
     halves = recv1.shape[1]
     part = piece // halves
-    chunks = recv2.shape[1]
+    chunks = left.shape[0]
+    cuts = recv2.shape[1] // chunks
+    units = chunks * cuts
+    cut_rows = pair_rows // cuts
     top = line - 1
     up, down, across, beside = me + 4, me - 4, me + 2 - 4 * y, me + 1 - 2 * k
     pending = []
@@ -142,19 +147,20 @@
     def arrive1(source, half):
         move1(source, half, 0, beside).wait_recv()
 
-    def move2(source, chunk, way, target):
-        rows = pl.ds(chunk * pair_rows, pair_rows)
+    def move2(source, chunk, bit, way, target):
+        rows = pl.ds(chunk * pair_rows + bit * cut_rows, cut_rows)
+        unit = chunk * cuts + bit
         return pltpu.make_async_remote_copy(
             src_ref=held.at[source, rows],
             dst_ref=held.at[source, rows],
-            send_sem=send2.at[way, source, chunk],
-            recv_sem=recv2.at[source, chunk],
+            send_sem=send2.at[way, source, unit],
+            recv_sem=recv2.at[source, unit],
             device_id={"panel": target},
             device_id_type=pl.DeviceIdType.MESH,
         )
 
-    def arrive2(source, chunk):
-        move2(source, chunk, 0, beside).wait_recv()
+    def arrive2(source, chunk, bit):
+        move2(source, chunk, bit, 0, beside).wait_recv()
 
     def move3(source, step, target):
         return pltpu.make_async_remote_copy(
@@ -166,11 +172,11 @@
             device_id_type=pl.DeviceIdType.MESH,
         )
 
-    def spread(condition, chunk, source, behind):
+    def spread(condition, chunk, bit, source, behind):
         side = (behind >= y) & (behind <= y + 1)
         near = behind <= 2
-        start(condition & side, move2(source, chunk, 2, across))
-        start(condition & near, move2(source, chunk, 3, beside))
+        start(condition & side, move2(source, chunk, bit, 2, across))
+        start(condition & near, move2(source, chunk, bit, 3, beside))
 
     def order(source, step):
         far = source // 4
@@ -191,10 +197,6 @@
     ]
     for copy in local:
         copy.start()
-    for pair in range(line):
-        place_masked(snps, scores.at[0, pl.ds(2 * pair, 2)], pair, masked.at[pair])
-    for copy in local:
-        copy.wait()
 
     def plane(index):
         rows = pl.ds(index * pair_rows, pair_rows)
@@ -236,13 +238,19 @@
             plane(z + sign * distance)
 
         chunk = z + sign * distance
-        start(has & (z < top), move2(me, chunk, 0, up))
-        start(has & (z >= line - 2), move2(me, chunk, 1, down))
-        spread(has, chunk, me, 0)
+        for bit in range(cuts):
+            start(has & (z < top), move2(me, chunk, bit, 0, up))
+            start(has & (z >= line - 2), move2(me, chunk, bit, 1, down))
+            spread(has, chunk, bit, me, 0)
 
     for distance in range(1, line + 1):
         if distance < line:
             column(distance)
+        if distance == 1:
+            for pair in range(line):
+                place_masked(snps, scores.at[0, pl.ds(2 * pair, 2)], pair, masked.at[pair])
+            for copy in local:
+                copy.wait()
         last = distance - 1
         signs = (1,) if last == 0 else (-1, 1)
         for sign in signs:
@@ -280,52 +288,54 @@
     near = [lax.rem(z - lag + line, line) * 4 + y * 2 + k for lag in range(3)]
     swap = 1 - 2 * k
 
-    for step in range(chunks + 2):
-        if step < chunks:
+    for unit in range(units + 2):
+        step, bit = unit // cuts, unit % cuts
+        if unit < units:
             for distance in range(1, line):
                 if distance <= 2:
                     has = z >= distance
                     source = me - 4 * distance
                     chunk = order(source, step)
-                    pl.when(has)(functools.partial(arrive2, source, chunk))
+                    pl.when(has)(functools.partial(arrive2, source, chunk, bit))
                     if distance == 1:
-                        start(has & (z < top), move2(source, chunk, 0, up))
-                    spread(has, chunk, source, distance)
+                        start(has & (z < top), move2(source, chunk, bit, 0, up))
+                    spread(has, chunk, bit, source, distance)
                 has = (z + distance <= top) & (z + distance >= line - 2)
                 source = me + 4 * distance
                 chunk = order(source, step)
-                pl.when(has)(functools.partial(arrive2, source, chunk))
-                start(has & (z > 0), move2(source, chunk, 1, down))
-                spread(has, chunk, source, line - distance)
-        if step == 0:
+                pl.when(has)(functools.partial(arrive2, source, chunk, bit))
+                start(has & (z > 0), move2(source, chunk, bit, 1, down))
+                spread(has, chunk, bit, source, line - distance)
+        if unit == 0:
             for number in range(1, others + 1):
                 move3(lax.rem(me + number, others + 1), number, beside).wait_recv()
             for index in range(chunks):
                 weigh(index)
-        if 0 < step <= chunks:
+        step, bit = (unit - 1) // cuts, (unit - 1) % cuts
+        if 0 < unit <= units:
             for source in cross:
-                chunk = order(source, step - 1)
-                arrive2(source, chunk)
-                start(None, move2(source, chunk, 3, beside))
-        if 0 < step <= chunks:
-            for lag, source in enumerate(near):
-                gram(source, order(source, step - 1), 4 * lag, lag == 0)
-            for lag, source in enumerate(cross):
-                gram(source, order(source, step - 1), 4 * lag + 2)
-        if step > 1:
-            for lag, source in enumerate(near):
-                chunk = order(source, step - 2)
-                arrive2(source + swap, chunk)
-                number = 4 * lag - swap
-
-                @pl.when((number >= 0) & (number < out.shape[0]))
-                def _():
-                    gram(source + swap, chunk, number)
-
-            for lag, source in enumerate(cross):
-                chunk = order(source, step - 2)
-                arrive2(source + swap, chunk)
-                gram(source + swap, chunk, 4 * lag + 2 - swap)
+                chunk = order(source, step)
+                arrive2(source, chunk, bit)
+                start(None, move2(source, chunk, bit, 3, beside))
+            if bit == cuts - 1:
+                for lag, source in enumerate(near):
+                    gram(source, order(source, step), 4 * lag, lag == 0)
+                for lag, source in enumerate(cross):
+                    gram(source, order(source, step), 4 * lag + 2)
+        step, bit = (unit - 2) // cuts, (unit - 2) % cuts
+        if unit > 1:
+            for source in near + cross:
+                arrive2(source + swap, order(source, step), bit)
+            if bit == cuts - 1:
+                for lag, source in enumerate(near):
+                    number = 4 * lag - swap
+
+                    @pl.when((number >= 0) & (number < out.shape[0]))
+                    def _():
+                        gram(source + swap, order(source, step), number)
+
+                for lag, source in enumerate(cross):
+                    gram(source + swap, order(source, step), 4 * lag + 2 - swap)
     for condition, copy in pending:
         if condition is None:
             copy.wait_send()
@@ -343,7 +353,8 @@
     rider = jnp.zeros((8, pair_rows), jnp.float32)
     spread = jnp.broadcast_to(values.astype(jnp.float32), (8, piece))
     rider = lax.dynamic_update_slice_in_dim(rider, spread, place, 1)
-    halves = 2
+    halves = HALVES
+    cuts = CUTS
     chunks = blocks // 2
     vmem = pl.BlockSpec(memory_space=pltpu.VMEM)
     smem = pl.BlockSpec(memory_space=pltpu.SMEM)
@@ -361,8 +372,8 @@
             pltpu.SemaphoreType.DMA((2,)),
             pltpu.SemaphoreType.DMA((4, devices, halves)),
             pltpu.SemaphoreType.DMA((devices, halves)),
-            pltpu.SemaphoreType.DMA((4, devices, chunks)),
-            pltpu.SemaphoreType.DMA((devices, chunks)),
+            pltpu.SemaphoreType.DMA((4, devices, chunks * cuts)),
+            pltpu.SemaphoreType.DMA((devices, chunks * cuts)),
             pltpu.SemaphoreType.DMA((devices,)),
             pltpu.SemaphoreType.DMA((devices,)),
         ],

time: 104 us -> 112 us (1.077)
  Pallas kernels: 95.6 us -> 104 us
    pallas_call x1, Pallas kernels: 95.6 us -> 104 us  [exchange(): pl.pallas_call(exchange_kernel, out_shape=jax.ShapeDtypeStruct((ROUNDS +...]
where the time goes in v5:
time: 112 us
  Pallas kernels  104 us (93%)
  other arithmetic  5.61 us (5%)
  local copies, waits for them, and re-layouts  2.11 us (2%)
    pallas_call x1, Pallas kernels, exchange(): pl.pallas_call(exchange_kernel, out_shape=jax.ShapeDtypeStruct((ROUNDS +...  104 us
    mul x1, other arithmetic, per_device(): return raw * scale[:, None, None]  5.43 us

profile of v5, /device:TPU:1, one launch (start us, length us, event | category | flops | bytes accessed | tf_op | source)
XLA Modules:
  0.0 111.8 jit_solution(8568123733545372363)
XLA Ops:
  0.0 0.0 copy-start.1
  0.0 0.7 broadcast_in_dim.5
  0.7 0.3 dynamic_update_slice.3.own_values
  0.9 0.0 copy-start
  0.9 0.6 copy-done
  1.5 104.1 %shard_map.64 = f32[9,1,8,128,128]{4,3,2,1,0:T(8,128)} custom-call(s32[8]{0:T(128)} %counts, s32[8]{0:T(128)} %snps, bf16[160,1024]{1,0:T(8,128)(2,1)} %own.1, f32[8,640]{1,0:T(8,128)} %copy-done, bf16[1,8,1024,128]{3,2,1,0:T(8,128)(2,1)} %scores.1), custom_call_target="tpu_custom_call" | custom-call | tf_op jit(solution)/shard_map/pallas_call | solution.py:361
  105.6 0.0 copy-done.1
  105.7 0.6 gather_fusion
  106.2 0.2 multiply_rsqrt_fusion
  106.4 5.4 %broadcast_multiply_fusion = f32[9,1,8,128,128]{4,3,2,1,0:T(8,128)} fusion(f32[9,1,8,128,128]{4,3,2,1,0:T(8,128)} %shard_map.64, f32[9,128,128]{2,1,0:T(8,128)S(1)} %multiply_rsqrt_fusion), kind=kLoop, calls=%fused_computation.1 | loop fusion | flops 1179648 | bytes 10027008 | tf_op jit(solution)/shard_map/mul | solution.py:404
  (5 shorter events, 0.0 us)
Async XLA Ops:
  0.0 105.6 %copy-start.1 = (bf16[2048]{0:T(1024)(128)(2,1)S(1)}, bf16[2048]{0:T(1024)(128)(2,1)}, u32[]{:S(2)}) copy-start(bf16[2048]{0:T(1024)(128)(2,1)} %param.11) | copy-start | bytes 12292
  0.9 0.6 copy-start

commit v6 on v5

--- a/solution.py
+++ b/solution.py
@@ -8,7 +8,7 @@
 from jax.sharding import PartitionSpec as P
 
 ROUNDS = 8
-HALVES = 5
+HALVES = 2
 CUTS = 2
 LIMIT = 56 * 1024 * 1024
 
@@ -198,6 +198,11 @@
     for copy in local:
         copy.start()
 
+    for pair in range(line):
+        place_masked(snps, scores.at[0, pl.ds(2 * pair, 2)], pair, masked.at[pair])
+    for copy in local:
+        copy.wait()
+
     def plane(index):
         rows = pl.ds(index * pair_rows, pair_rows)
         held[me, rows] = project_rows(store[rows], masked[index], counts[2 * index])
@@ -246,11 +251,6 @@
     for distance in range(1, line + 1):
         if distance < line:
             column(distance)
-        if distance == 1:
-            for pair in range(line):
-                place_masked(snps, scores.at[0, pl.ds(2 * pair, 2)], pair, masked.at[pair])
-            for copy in local:
-                copy.wait()
         last = distance - 1
         signs = (1,) if last == 0 else (-1, 1)
         for sign in signs:

time: 112 us -> 110 us (0.982)
  Pallas kernels: 104 us -> 102 us
    pallas_call x1, Pallas kernels: 104 us -> 102 us  [exchange(): pl.pallas_call(exchange_kernel, out_shape=jax.ShapeDtypeStruct((ROUNDS +...]
where the time goes in v6:
time: 110 us; the launch traced here: 109 us
  Pallas kernels  102 us (93%)
  other arithmetic  5.61 us (5%)
  local copies, waits for them, and re-layouts  2.11 us (2%)
    pallas_call x1, Pallas kernels, exchange(): pl.pallas_call(exchange_kernel, out_shape=jax.ShapeDtypeStruct((ROUNDS +...  102 us
    mul x1, other arithmetic, per_device(): return raw * scale[:, None, None]  5.43 us

profile of v6, /device:TPU:1, one launch (start us, length us, event | category | flops | bytes accessed | tf_op | source)
XLA Modules:
  0.0 109.4 jit_solution(6876492782830342953)
XLA Ops:
  0.0 0.0 copy-start.1
  0.0 0.7 broadcast_in_dim.5
  0.7 0.3 dynamic_update_slice.3.own_values
  0.9 0.0 copy-start
  0.9 0.6 copy-done
  1.5 101.6 %shard_map.64 = f32[9,1,8,128,128]{4,3,2,1,0:T(8,128)} custom-call(s32[8]{0:T(128)} %counts, s32[8]{0:T(128)} %snps, bf16[160,1024]{1,0:T(8,128)(2,1)} %own.1, f32[8,640]{1,0:T(8,128)} %copy-done, bf16[1,8,1024,128]{3,2,1,0:T(8,128)(2,1)} %scores.1), custom_call_target="tpu_custom_call" | custom-call | tf_op jit(solution)/shard_map/pallas_call | solution.py:361
  103.2 0.0 copy-done.1
  103.2 0.6 gather_fusion
  103.8 0.2 multiply_rsqrt_fusion
  104.0 5.4 %broadcast_multiply_fusion = f32[9,1,8,128,128]{4,3,2,1,0:T(8,128)} fusion(f32[9,1,8,128,128]{4,3,2,1,0:T(8,128)} %shard_map.64, f32[9,128,128]{2,1,0:T(8,128)S(1)} %multiply_rsqrt_fusion), kind=kLoop, calls=%fused_computation.1 | loop fusion | flops 1179648 | bytes 10027008 | tf_op jit(solution)/shard_map/mul | solution.py:404
  (5 shorter events, 0.0 us)
Async XLA Ops:
  0.0 103.2 %copy-start.1 = (bf16[2048]{0:T(1024)(128)(2,1)S(1)}, bf16[2048]{0:T(1024)(128)(2,1)}, u32[]{:S(2)}) copy-start(bf16[2048]{0:T(1024)(128)(2,1)} %param.11) | copy-start | bytes 12292
  0.9 0.6 copy-start
